TPU v7x, 128 devices: a whole 4x4x4 slice. The times are simulated.
128 devices in a mesh: row: 8 (over x_hi, z), col: 16 (over x_lo, y, core).
Axes of the slice: x: 4 (x_hi: 2, x_lo: 2; x = x_hi * 2 + x_lo), y: 4, z: 4, core: 2. Of those that a mesh axis runs over, the one named last changes fastest.
Arguments:
- tokens: bfloat16 [4096, 2048], P(('row', 'col')), may hold values from -6 to 6
- routes: int32 [4096, 6], P(('row', 'col')), may hold values from 0 to 63, as said below
- router: bfloat16 [2048, 64], replicated, may hold values from -0.125 to 0.125
- w_in: bfloat16 [128, 2048, 1408], P(('row', 'col')), may hold values from -0.125 to 0.125
- w_out: bfloat16 [128, 704, 2048], P(('row', 'col')), may hold values from -0.15625 to 0.15625
- cache_prefill: bfloat16 [9216, 9216], P(('row', 'col')), may hold values from -6 to 6
- page_slot: int32 [9216], P(('row', 'col')), may hold values from 0 to 9215, as said below
Outputs:
- moe_out: bfloat16 [4096, 2048], P(('row', 'col'))
- cache_decode: bfloat16 [9216, 9216], P(('row', 'col'))
Inputs may be any that keep to these rules, and one draw needn't show every extreme that they name: `routes`: each row names 6 different experts. In the rows of one device no expert is named more than 6 times, and one expert, the same for all devices, is named exactly 6 times in every device's rows. `page_slot`: A permutation of the page rows. Every device receives exactly 72 pages; at most 1 pages go from one device to one device, and some pair of devices reaches 1.
All inputs are finite; a program needn't handle non-finite values.
Results may differ from a plain program's by a relative error of at most 0.0065.
Values may be sent and summed in bfloat16 or wider, within the bound.
No kernel may reach another device: no remote copies, remote signals or barrier semaphores. Data moves between devices by JAX's collectives and lax.ppermute only.
A program may use at most 128 MiB of HBM per device.

v0:
```python
import jax
import jax.numpy as jnp
from jax import lax
from jax.sharding import PartitionSpec as P

EXPERTS = 64
CAPE = 6


route_scale = 2.446


def gate_values_of(tokens, routes, router):
    logits = jnp.dot(tokens, router, preferred_element_type=jnp.float32)
    scores = jax.nn.sigmoid(logits)
    picked = jnp.take_along_axis(scores, routes, axis=1)
    return route_scale * picked / jnp.sum(picked, axis=1, keepdims=True)


def expert_halves(buffer, w_in, w_out):
    gate_up = jnp.einsum("ajcd,jdf->ajcf", buffer, w_in, preferred_element_type=jnp.float32)
    hidden_width = w_out.shape[1]
    activated = (jax.nn.silu(gate_up[..., :hidden_width]) * gate_up[..., hidden_width:]).astype(
        jnp.bfloat16
    )
    return jnp.einsum(
        "ajcf,jfd->ajcd", activated, w_out, preferred_element_type=jnp.float32
    ).astype(jnp.bfloat16)


def move_pages(cache_prefill, page_slot):
    devices = lax.axis_size("row") * lax.axis_size("col")
    pages_here, page_width = cache_prefill.shape
    page_cap = pages_here // devices + 1
    target = page_slot // pages_here
    within = page_slot % pages_here
    onehot_dest = (target[:, None] == jnp.arange(devices, dtype=jnp.int32)[None, :]).astype(
        jnp.int32
    )
    before = jnp.cumsum(onehot_dest, axis=0) - onehot_dest
    ranking = jnp.sum(before * onehot_dest, axis=1)
    placed = target * page_cap + ranking
    source_of = (
        jnp.full((devices * page_cap,), pages_here, jnp.int32)
        .at[placed]
        .set(jnp.arange(pages_here, dtype=jnp.int32))
    )
    landing = jnp.full((devices * page_cap,), pages_here, jnp.int32).at[placed].set(within)
    extended = jnp.concatenate(
        [cache_prefill, jnp.zeros((1, page_width), cache_prefill.dtype)], axis=0
    )
    outgoing = extended[source_of].reshape(devices, page_cap, page_width)
    arrived, arrived_slot = (
        lax.all_to_all(outgoing, ("row", "col"), split_axis=0, concat_axis=0, tiled=True),
        lax.all_to_all(
            landing.reshape(devices, page_cap),
            ("row", "col"),
            split_axis=0,
            concat_axis=0,
            tiled=True,
        ),
    )
    placed_rows = (
        jnp.zeros_like(extended).at[arrived_slot.reshape(-1)].set(arrived.reshape(-1, page_width))
    )
    return placed_rows[:pages_here]


def per_device(tokens, routes, router, w_in, w_out, cache_prefill, page_slot):
    cache_decode = move_pages(cache_prefill, page_slot)
    devices = lax.axis_size("row") * lax.axis_size("col")
    tok_count, model_width = tokens.shape
    top_count = routes.shape[1]
    halves_here = w_in.shape[0]
    gate_values = gate_values_of(tokens, routes, router)
    flat_routes = routes.reshape(-1)
    onehot_expert = (flat_routes[:, None] == jnp.arange(EXPERTS, dtype=jnp.int32)[None, :]).astype(
        jnp.int32
    )
    ranking = jnp.sum((jnp.cumsum(onehot_expert, axis=0) - onehot_expert) * onehot_expert, axis=1)
    slot_index = flat_routes * CAPE + ranking
    token_of = jnp.arange(tok_count * top_count, dtype=jnp.int32) // top_count
    slot_token = jnp.full((EXPERTS * CAPE,), tok_count, jnp.int32).at[slot_index].set(token_of)
    extended = jnp.concatenate([tokens, jnp.zeros((1, model_width), tokens.dtype)], axis=0)
    slot_rows = extended[slot_token]
    outgoing = jnp.broadcast_to(slot_rows[None], (2,) + slot_rows.shape)
    outgoing = outgoing.reshape(devices, halves_here, CAPE, model_width)
    returned = lax.all_to_all(
        expert_halves(
            lax.all_to_all(outgoing, ("row", "col"), split_axis=0, concat_axis=0, tiled=True),
            w_in,
            w_out,
        ),
        ("row", "col"),
        split_axis=0,
        concat_axis=0,
        tiled=True,
    )
    returned = returned.reshape(2, EXPERTS * CAPE, model_width)
    expert_out = (returned[0].astype(jnp.float32) + returned[1].astype(jnp.float32)).astype(
        jnp.bfloat16
    )
    picked_out = (
        expert_out[slot_index].reshape(tok_count, top_count, model_width).astype(jnp.float32)
    )
    moe_out = jnp.sum(picked_out * gate_values[:, :, None], axis=1).astype(jnp.bfloat16)
    return (moe_out, cache_decode)


def solution(mesh):
    in_specs = (
        P(("row", "col"), None),
        P(("row", "col"), None),
        P(),
        P(("row", "col"), None, None),
        P(("row", "col"), None, None),
        P(("row", "col"), None),
        P(("row", "col")),
    )
    out_specs = (P(("row", "col"), None), P(("row", "col"), None))
    return jax.shard_map(
        per_device, mesh=mesh, in_specs=in_specs, out_specs=out_specs, check_vma=False
    )
```

profile of v0, /device:TPU:0, one launch (start us, length us, event | category | flops | bytes accessed | tf_op | source)
XLA Modules:
  0.0 211.7 jit_solution(16359055763036879707)
XLA Ops:
  0.6 0.8 and_select_fusion.1
  1.5 0.1 reduce_window_sum.28
  1.7 0.2 select_reduce_fusion
  1.8 0.8 scatter_custom_fusion.1
  2.7 0.7 copy.45
  3.4 11.1 %all-to-all-start.2 = ((s32[128,1,1]{2,1,0:T(1,128)}), s32[128,1,1]{2,1,0:T(1,128)S(1)}, u32[]{:S(2)}, u32[]{:S(2)}) async-start(s32[128,1,1]{2,1,0:T(1,128)} %copy.45), calls=%async_computation.2 | async-start | bytes 131072 | tf_op jit(solution)/shard_map/all_to_all | solution.py:55
  14.5 0.8 copy.35
  15.3 0.7 broadcast_multiply_fusion
  16.0 0.1 eq.37
  16.2 0.6 reduce-window.6
  16.8 0.2 slice_reduce_fusion
  17.0 0.1 bitcast_bitcast_fusion
  17.1 0.1 copy.34
  17.2 0.1 mul.49
  17.3 1.2 scatter_custom_fusion
  18.6 0.9 concatenate.6
  19.5 3.1 %gather_fusion = bf16[384,2048]{1,0:T(8,128)(2,1)} fusion(bf16[33,2048]{1,0:T(8,128)(2,1)S(1)} %concatenate.6, s32[1024]{0:T(1024)S(1)} %pad_clamp_fusion.2), kind=kCustom, calls=%fused_computation | custom fusion | bytes 3147264 | tf_op jit(solution)/shard_map/gather | solution.py:85
  22.6 3.5 %broadcast_in_dim.18 = bf16[2,384,2048]{2,1,0:T(8,128)(2,1)} broadcast(bf16[384,2048]{1,0:T(8,128)(2,1)} %gather_fusion), dimensions={1,2} | broadcast | bytes 4718592 | tf_op jit(solution)/shard_map/broadcast_in_dim | solution.py:86
  26.1 6.3 %reshape.138 = bf16[128,1,6,2048]{3,2,0,1:T(8,128)(2,1)} reshape(bf16[2,384,2048]{2,1,0:T(8,128)(2,1)} %broadcast_in_dim.18) | data formatting | bytes 6291456 | tf_op jit(solution)/shard_map/reshape | solution.py:87
  32.3 10.3 %all-to-all-start = ((bf16[128,1,6,2048]{3,2,1,0:T(8,128)(2,1)}), bf16[128,1,6,2048]{3,2,1,0:T(8,128)(2,1)}, u32[]{:S(2)}, u32[]{:S(2)}) async-start(bf16[128,1,6,2048]{3,2,1,0:T(8,128)(2,1)} %bitcast.58), calls=%async_computation | async-start | bytes 8388608 | tf_op jit(solution)/shard_map/all_to_all | solution.py:90
  42.7 0.8 scatter_custom_fusion.2
  43.5 2.6 %concatenate.7 = bf16[73,9216]{1,0:T(8,128)(2,1)} pad(bf16[72,9216]{1,0:T(8,128)(2,1)} %param.12, bf16[]{:T(256)} %constant.34.clone.1), padding=0_1x0_0 | pad | bytes 2672642 | tf_op jit(solution)/shard_map/concatenate | solution.py:49
  46.0 7.2 %gather_fusion.2 = bf16[128,9216]{1,0:T(8,128)(2,1)} fusion(bf16[73,9216]{1,0:T(8,128)(2,1)} %concatenate.7, s32[1024]{0:T(1024)S(1)} %pad_clamp_fusion), kind=kCustom, calls=%fused_computation.2 | custom fusion | bytes 4719104 | tf_op jit(solution)/shard_map/gather | solution.py:52
  53.2 0.5 broadcast.170
  53.7 4.7 %reduce.3 = bf16[128,9216]{1,0:T(8,128)(2,1)} reduce(bf16[128,1,9216]{2,0,1:T(8,128)(2,1)} %bitcast.59, bf16[]{:T(256)} %broadcast.170), dimensions={1}, to_apply=%copy.46.reduce_sub_computation | reduce | bytes 4718594 | tf_op jit(solution)/shard_map/reshape | solution.py:52
  58.5 4.7 %reshape.231 = bf16[128,2,4608]{2,1,0:T(2,128)(2,1)} reshape(bf16[128,9216]{1,0:T(8,128)(2,1)} %reduce.3) | data formatting | bytes 4718592
  63.2 32.0 %all-to-all-done = bf16[128,1,6,2048]{3,2,1,0:T(8,128)(2,1)} async-done(((bf16[128,1,6,2048]{3,2,1,0:T(8,128)(2,1)}), bf16[128,1,6,2048]{3,2,1,0:T(8,128)(2,1)}, u32[]{:S(2)}, u32[]{:S(2)}) %all-to-all-start) | async-done | bytes 3145760 | tf_op jit(solution)/shard_map/all_to_all | solution.py:90
  95.2 7.0 %all-to-all-start.3 = ((bf16[128,2,4608]{2,1,0:T(2,128)(2,1)}), bf16[128,2,4608]{2,1,0:T(2,128)(2,1)}, u32[]{:S(2)}, u32[]{:S(2)}) async-start(bf16[128,2,4608]{2,1,0:T(2,128)(2,1)} %reshape.231), calls=%async_computation.3 | async-start | bytes 4718592 | tf_op jit(solution)/shard_map/all_to_all | solution.py:54
  102.2 12.5 %fusion.2 = f32[128,1,6,1408]{3,0,2,1:T(8,128)S(1)} fusion(bf16[1,2048,1408]{2,1,0:T(8,128)(2,1)} %param.10, bf16[128,1,6,2048]{3,2,1,0:T(8,128)(2,1)} %all-to-all-done), kind=kOutput, calls=%fused_computation.11 | convolution fusion | flops 4429185024 | bytes 13238272 | tf_op jit(solution)/shard_map/ajcd,jdf->ajcf/dot_general | solution.py:21
  114.8 3.0 %fusion.7 = bf16[128,1,6,2048]{3,0,2,1:T(8,128)(2,1)S(1)} fusion(bf16[1,704,2048]{2,1,0:T(8,128)(2,1)S(1)} %copy-done, f32[128,1,6,1408]{3,0,2,1:T(8,128)S(1)} %fusion.2), kind=kOutput, calls=%fused_computation.15 | convolution fusion | flops 2219409408 | bytes 10747904 | tf_op jit(solution)/shard_map/ajcf,jfd->ajcd/dot_general | solution.py:26
  117.8 3.7 %copy.41 = bf16[128,1,6,2048]{3,2,1,0:T(8,128)(2,1)} copy(bf16[128,1,6,2048]{3,0,2,1:T(8,128)(2,1)S(1)} %fusion.7) | data formatting | bytes 6291456 | tf_op jit(solution)/shard_map/convert_element_type | solution.py:28
  121.5 13.5 %all-to-all-done.3 = bf16[128,2,4608]{2,1,0:T(2,128)(2,1)} async-done(((bf16[128,2,4608]{2,1,0:T(2,128)(2,1)}), bf16[128,2,4608]{2,1,0:T(2,128)(2,1)}, u32[]{:S(2)}, u32[]{:S(2)}) %all-to-all-start.3) | async-done | bytes 2359328 | tf_op jit(solution)/shard_map/all_to_all | solution.py:54
  135.0 6.0 %all-to-all-start.1 = ((bf16[128,1,6,2048]{3,2,1,0:T(8,128)(2,1)}), bf16[128,1,6,2048]{3,2,1,0:T(8,128)(2,1)}, u32[]{:S(2)}, u32[]{:S(2)}) async-start(bf16[128,1,6,2048]{3,2,1,0:T(8,128)(2,1)} %copy.41), calls=%async_computation.1 | async-start | bytes 8388608 | tf_op jit(solution)/shard_map/all_to_all | solution.py:88
  141.1 0.1 reshape.172
  141.2 0.2 fusion.17
  141.4 1.6 gather_fusion.3
  143.0 0.1 reshape.175
  143.1 0.1 fusion.22
  143.3 2.4 %reduce.1 = s32[128]{0:T(128)S(1)} reduce(s32[128,1,1]{2,1,0:T(1,128)S(1)} %all-to-all-done.2, s32[]{:T(128)} %constant.44.clone.1), dimensions={1,2}, to_apply=%all_to_all.20.reduce_sub_computation | reduce | bytes 1028 | tf_op jit(solution)/shard_map/all_to_all | solution.py:55
  145.7 14.4 %reshape.232 = bf16[128,1,9216]{2,1,0:T(2,128)(2,1)} reshape(bf16[128,2,4608]{2,1,0:T(2,128)(2,1)} %all-to-all-done.3) | data formatting | bytes 4718592
  160.2 7.3 %scatter_custom_fusion.3 = bf16[73,9216]{1,0:T(8,128)(2,1)} fusion(s32[128]{0:T(128)S(1)} %fusion.25, bf16[128,1,9216]{2,1,0:T(2,128)(2,1)} %reshape.232, bf16[]{:T(256)} %constant.34.clone.1), kind=kCustom, calls=%fused_computation.19 | custom fusion | bytes 3704834 | tf_op jit(solution)/shard_map/scatter | solution.py:64
  167.5 2.5 %slice.48 = bf16[72,9216]{1,0:T(8,128)(2,1)} slice(bf16[73,9216]{1,0:T(8,128)(2,1)} %scatter_custom_fusion.3), slice={[0:72], [0:9216]} | slice | bytes 2654208 | tf_op jit(solution)/shard_map/slice | solution.py:66
  169.9 23.4 %all-to-all-done.1 = bf16[128,1,6,2048]{3,2,1,0:T(8,128)(2,1)} async-done(((bf16[128,1,6,2048]{3,2,1,0:T(8,128)(2,1)}), bf16[128,1,6,2048]{3,2,1,0:T(8,128)(2,1)}, u32[]{:S(2)}, u32[]{:S(2)}) %all-to-all-start.1) | async-done | bytes 3145760 | tf_op jit(solution)/shard_map/all_to_all | solution.py:88
  193.4 4.7 %add_convert_fusion = bf16[64,1,6,2048]{3,2,1,0:T(8,128)(2,1)} fusion(bf16[128,1,6,2048]{3,2,1,0:T(8,128)(2,1)} %all-to-all-done.1), kind=kLoop, calls=%fused_computation.10 | loop fusion | flops 3145728 | bytes 4718592 | tf_op jit(solution)/shard_map/convert_element_type | solution.py:100
  198.1 3.7 %convert_element_type.54 = bf16[384,2048]{1,0:T(8,128)(2,1)} reshape(bf16[64,1,6,2048]{3,2,1,0:T(8,128)(2,1)} %add_convert_fusion) | data formatting | bytes 3145728 | tf_op jit(solution)/shard_map/convert_element_type | solution.py:100
  201.9 4.4 %gather_fusion.1 = bf16[192,2048]{1,0:T(8,128)(2,1)} fusion(bf16[384,2048]{1,0:T(8,128)(2,1)} %convert_element_type.54, s32[1024]{0:T(1024)S(1)} %pad_clamp_fusion.1), kind=kCustom, calls=%fused_computation.1 | custom fusion | bytes 1573632 | tf_op jit(solution)/shard_map/gather | solution.py:104
  206.3 2.5 %reshape.147 = f32[32,6,2048]{2,1,0:T(8,128)} reshape(bf16[192,2048]{1,0:T(8,128)(2,1)} %gather_fusion.1) | data formatting | bytes 2359296 | tf_op jit(solution)/shard_map/convert_element_type | solution.py:104
  208.7 3.0 %multiply_reduce_fusion = bf16[32,2048]{1,0:T(8,128)(2,1)} fusion(f32[32,6,2048]{2,1,0:T(8,128)} %reshape.147, f32[32,6]{1,0:T(8,128)S(1)} %multiply_divide_fusion), kind=kLoop, calls=%fused_computation.22 | loop fusion | flops 720896 | bytes 1704704 | tf_op jit(solution)/shard_map/reduce_sum | solution.py:106
  (25 shorter events, 0.3 us)
Async XLA Ops:
  0.6 114.1 %copy-start = (bf16[1,704,2048]{2,1,0:T(8,128)(2,1)S(1)}, bf16[1,704,2048]{2,1,0:T(8,128)(2,1)}, u32[]{:S(2)}) copy-start(bf16[1,704,2048]{2,1,0:T(8,128)(2,1)} %param.11) | copy-start | bytes 8650756
  3.4 28.9 %all-to-all-start.2 = ((s32[128,1,1]{2,1,0:T(1,128)}), s32[128,1,1]{2,1,0:T(1,128)S(1)}, u32[]{:S(2)}, u32[]{:S(2)}) async-start(s32[128,1,1]{2,1,0:T(1,128)} %copy.45), calls=%async_computation.2 | async-start | bytes 131072 | tf_op jit(solution)/shard_map/all_to_all | solution.py:55
  32.3 62.8 %all-to-all-start = ((bf16[128,1,6,2048]{3,2,1,0:T(8,128)(2,1)}), bf16[128,1,6,2048]{3,2,1,0:T(8,128)(2,1)}, u32[]{:S(2)}, u32[]{:S(2)}) async-start(bf16[128,1,6,2048]{3,2,1,0:T(8,128)(2,1)} %bitcast.58), calls=%async_computation | async-start | bytes 8388608 | tf_op jit(solution)/shard_map/all_to_all | solution.py:90
  95.2 39.8 %all-to-all-start.3 = ((bf16[128,2,4608]{2,1,0:T(2,128)(2,1)}), bf16[128,2,4608]{2,1,0:T(2,128)(2,1)}, u32[]{:S(2)}, u32[]{:S(2)}) async-start(bf16[128,2,4608]{2,1,0:T(2,128)(2,1)} %reshape.231), calls=%async_computation.3 | async-start | bytes 4718592 | tf_op jit(solution)/shard_map/all_to_all | solution.py:54
  121.5 19.7 %copy-start.1 = (bf16[32,2048]{1,0:T(8,128)(2,1)S(1)}, bf16[32,2048]{1,0:T(8,128)(2,1)}, u32[]{:S(2)}) copy-start(bf16[32,2048]{1,0:T(8,128)(2,1)} %param.7) | copy-start | bytes 393220
  121.5 19.7 %copy-start.2 = (bf16[2048,64]{0,1:T(8,128)(2,1)S(1)}, bf16[2048,64]{0,1:T(8,128)(2,1)}, u32[]{:S(2)}) copy-start(bf16[2048,64]{0,1:T(8,128)(2,1)} %param.9) | copy-start | bytes 786436
  135.0 58.4 %all-to-all-start.1 = ((bf16[128,1,6,2048]{3,2,1,0:T(8,128)(2,1)}), bf16[128,1,6,2048]{3,2,1,0:T(8,128)(2,1)}, u32[]{:S(2)}, u32[]{:S(2)}) async-start(bf16[128,1,6,2048]{3,2,1,0:T(8,128)(2,1)} %copy.41), calls=%async_computation.1 | async-start | bytes 8388608 | tf_op jit(solution)/shard_map/all_to_all | solution.py:88
where the time goes:
time: 214 us; the launch traced here: 212 us
  local copies, waits for them, and re-layouts  73.9 us (35%)
  waiting for transfers between devices  68.9 us (32%)
  starting transfers between devices  34.5 us (16%)
  other arithmetic  17.8 us (8%)
  matrix products  15.7 us (7%)
    all_to_all x1, waiting for transfers between devices, per_device(): lax.all_to_all(outgoing, ('row', 'col'), split_axis=0, concat_axis=0, til...  32 us
    all_to_all x1, waiting for transfers between devices, per_device(): lax.all_to_all(expert_halves(lax.all_to_all(outgoing, ('row', 'col'), spl...  23.4 us
    unnamed x9, local copies, waits for them, and re-layouts  19.9 us
    all_to_all x1, waiting for transfers between devices, move_pages(): lax.all_to_all(outgoing, ('row', 'col'), split_axis=0, concat_axis=0, til...  13.5 us
    dot_general x1, matrix products, expert_halves(): jnp.einsum('ajcd,jdf->ajcf', buffer, w_in, preferred_element_type=jnp.flo...  12.5 us
    all_to_all x1, starting transfers between devices, move_pages(): lax.all_to_all(landing.reshape(devices, page_cap), ('row', 'col'), split_...  11.1 us
    all_to_all x1, starting transfers between devices, per_device(): lax.all_to_all(outgoing, ('row', 'col'), split_axis=0, concat_axis=0, til...  10.3 us
    scatter x1, local copies, waits for them, and re-layouts, move_pages(): jnp.zeros_like(extended).at[arrived_slot.reshape(-1)]  7.32 us
  transfers between devices with their start and end apart: 4, of which 3 were waited for; matrix products, arithmetic and copies ran while one was open for 41% of the time, Pallas kernels for 0%

commit v1 on v0

v1 whole, which is shorter than its diff:
```python
import functools

import jax
import jax.numpy as jnp
from jax import lax
from jax.experimental import pallas as pl
from jax.experimental.pallas import tpu as pltpu
from jax.sharding import PartitionSpec as P

EXPERTS = 64
CAPE = 6
ROUTE_SCALE = 2.446
AXES = ("row", "col")
BF = jnp.bfloat16
F32 = jnp.float32
VM = pl.BlockSpec(memory_space=pltpu.VMEM)


UNITS = 3


def iota(shape, dim):
    return lax.broadcasted_iota(jnp.int32, shape, dim)


def onehot(cond):
    return jnp.where(cond, 1.0, 0.0).astype(BF)


def dispatch_kernel(routes_ref, tok_ref, out_ref):
    tok = tok_ref.shape[0]
    rows = out_ref.shape[0] // 2
    unit = out_ref.shape[1] // UNITS
    row = iota((rows, tok), 0)
    expert, sub = row >> 3, row & 7
    named = routes_ref[0:1, :] == expert
    for k in range(1, routes_ref.shape[0]):
        named = named | (routes_ref[k : k + 1, :] == expert)
    before = onehot(iota((tok, tok), 0) < iota((tok, tok), 1))
    rank = jnp.dot(onehot(named), before, preferred_element_type=F32).astype(jnp.int32)
    rank = jnp.where(named, rank, 99)
    main = onehot(rank == sub)
    last = tok_ref[:, UNITS * unit :]
    for u in range(UNITS):
        tail = onehot((sub >= CAPE) & (rank == sub + (2 * u - CAPE)))
        picked = jnp.dot(main, tok_ref[:, u * unit : (u + 1) * unit], preferred_element_type=F32)
        picked = picked + jnp.dot(tail, last, preferred_element_type=F32)
        picked = picked.astype(BF)
        out_ref[0:rows, u * unit : (u + 1) * unit] = picked
        out_ref[rows : 2 * rows, u * unit : (u + 1) * unit] = picked


def dispatch(routes_t, tokens):
    width = tokens.shape[1]
    return pl.pallas_call(
        dispatch_kernel,
        out_shape=jax.ShapeDtypeStruct((2 * EXPERTS * 8, width * CAPE // 8), BF),
        in_specs=[VM, VM],
        out_specs=VM,
        compiler_params=pltpu.CompilerParams(vmem_limit_bytes=24 << 20),
        cost_estimate=pl.CostEstimate(flops=10**8, bytes_accessed=4 * 10**6, transcendentals=0),
        name="dispatch",
    )(routes_t, tokens)


def gates_kernel(routes_ref, tok_ref, router_ref, out_ref):
    tok = tok_ref.shape[0]
    cols = out_ref.shape[1]
    logits = lax.dot_general(
        tok_ref[...], router_ref[...], (((1,), (1,)), ((), ())), preferred_element_type=F32
    )
    scores = jax.nn.sigmoid(logits)
    expert = iota((EXPERTS, tok), 0)
    named = routes_ref[0:1, :] == expert
    for k in range(1, routes_ref.shape[0]):
        named = named | (routes_ref[k : k + 1, :] == expert)
    unit = onehot(iota((tok, tok), 0) == iota((tok, tok), 1))
    mine = lax.dot_general(
        unit, onehot(named), (((1,), (1,)), ((), ())), preferred_element_type=F32
    )
    before = onehot(iota((tok, tok), 1) < iota((tok, tok), 0))
    rank = jnp.dot(before, mine.astype(BF), preferred_element_type=F32)
    rank = jnp.where(mine > 0.5, rank, 99.0)
    picked = jnp.where(mine > 0.5, scores, 0.0)
    gate = ROUTE_SCALE * picked / jnp.sum(picked, axis=1, keepdims=True)
    high = gate.astype(BF)
    low = (gate - high.astype(F32)).astype(BF)
    spread = onehot(((iota((EXPERTS, cols), 1) >> 3) & (EXPERTS - 1)) == iota((EXPERTS, cols), 0))
    rank = jnp.dot(rank.astype(BF), spread, preferred_element_type=F32).astype(jnp.int32)
    high = jnp.dot(high, spread, preferred_element_type=F32)
    low = jnp.dot(low, spread, preferred_element_type=F32)
    sub = iota((tok, cols), 1) & 7
    for u in range(UNITS + 1):
        if u == 0:
            keep = rank == sub
        else:
            keep = (sub >= CAPE) & (rank == sub + (2 * (u - 1) - CAPE))
        out_ref[2 * u * tok : (2 * u + 1) * tok, :] = jnp.where(keep, high, 0.0).astype(BF)
        out_ref[(2 * u + 1) * tok : (2 * u + 2) * tok, :] = jnp.where(keep, low, 0.0).astype(BF)


def gates(routes_t, tokens, router_t):
    tok = tokens.shape[0]
    return pl.pallas_call(
        gates_kernel,
        out_shape=jax.ShapeDtypeStruct((2 * (UNITS + 1) * tok, 2 * EXPERTS * 8), BF),
        in_specs=[VM, VM, VM],
        out_specs=VM,
        cost_estimate=pl.CostEstimate(flops=10**8, bytes_accessed=2 * 10**6, transcendentals=0),
        name="gates",
    )(routes_t, tokens, router_t)


def pages_out_kernel(slot_ref, cache_ref, out_ref, stack_ref):
    pages, width = cache_ref.shape
    rows, chunk = out_ref.shape
    for c in range(8):
        stack_ref[c * 128 : c * 128 + pages, :] = cache_ref[:, c * chunk : (c + 1) * chunk]
        stack_ref[c * 128 + pages : (c + 1) * 128, :] = jnp.zeros((128 - pages, chunk), BF)
    step = 256
    for b in range(rows // step):
        row = iota((step, 1024), 0) + b * step
        first = (row >> 3) * pages
        slot = slot_ref[...]
        hit = (slot >= first) & (slot < first + pages)
        hit = hit & ((iota((step, 1024), 1) >> 7) == (row & 7))
        got = jnp.dot(onehot(hit), stack_ref[...], preferred_element_type=F32)
        out_ref[b * step : (b + 1) * step, :] = got.astype(BF)


def pages_out(slot_row, cache, devices):
    width = cache.shape[1]
    return pl.pallas_call(
        pages_out_kernel,
        out_shape=jax.ShapeDtypeStruct((devices * 8, width // 8), BF),
        in_specs=[VM, VM],
        out_specs=VM,
        scratch_shapes=[pltpu.VMEM((1024, width // 8), BF)],
        compiler_params=pltpu.CompilerParams(vmem_limit_bytes=40 << 20),
        cost_estimate=pl.CostEstimate(flops=2 * 10**9, bytes_accessed=4 * 10**6, transcendentals=0),
        name="pages_out",
    )(slot_row, cache)


def pages_in_kernel(first_ref, slots_ref, got_ref, out_ref):
    pages, width = out_ref.shape
    rows, chunk = got_ref.shape
    devices = slots_ref.shape[0]
    local = slots_ref[...] - first_ref[0]
    hit = (local >= 0) & (local < pages)
    local = jnp.sum(jnp.where(hit, local + 1, 0), axis=1, keepdims=True).astype(F32)
    spread = (iota((devices, rows), 1) >> 3) == iota((devices, rows), 0)
    table = jnp.where(spread, local, 0.0).astype(BF)
    ones = jnp.ones((8, devices), BF)
    line = jnp.dot(ones, table, preferred_element_type=F32)[0:1, :].astype(jnp.int32)
    pad = -(-pages // 16) * 16
    sub = iota((pad, rows), 1) & 7
    same = line == iota((pad, rows), 0) + 1
    pick = jnp.concatenate([onehot(same & (sub == c)) for c in range(8)], axis=0)
    placed = jnp.dot(pick, got_ref[...], preferred_element_type=F32)
    for c in range(8):
        out_ref[:, c * chunk : (c + 1) * chunk] = placed[c * pad : c * pad + pages, :].astype(BF)


def pages_in(first, slots, got, pages):
    rows, chunk = got.shape
    return pl.pallas_call(
        pages_in_kernel,
        out_shape=jax.ShapeDtypeStruct((pages, chunk * 8), BF),
        in_specs=[pl.BlockSpec(memory_space=pltpu.SMEM), VM, VM],
        out_specs=VM,
        compiler_params=pltpu.CompilerParams(vmem_limit_bytes=40 << 20),
        cost_estimate=pl.CostEstimate(flops=2 * 10**9, bytes_accessed=4 * 10**6, transcendentals=0),
        name="pages_in",
    )(first, slots, got)


def experts_kernel(x_ref, w_in_ref, w_out_ref, out_ref):
    rows, packed = x_ref.shape
    unit = packed // UNITS
    hidden = w_out_ref.shape[0]
    block = 128
    row, col = iota((block, UNITS * block), 0), iota((block, UNITS * block), 1)
    sub = row & 7
    inner = col & (block - 1)
    gather = onehot(
        (sub < CAPE)
        & ((row >> 3) == (inner >> 3))
        & ((col >> 7) == (sub >> 1))
        & ((inner & 7) == CAPE + (sub & 1))
    )
    row, col = iota((UNITS * block, block), 0), iota((UNITS * block, block), 1)
    sub = row & 7
    scatter = onehot(
        (sub >= CAPE)
        & (((row & (block - 1)) >> 3) == (col >> 3))
        & ((col & 7) == 2 * (row >> 7) + sub - CAPE)
    )
    tails = []
    for b in range(rows // block):
        part = x_ref[b * block : (b + 1) * block, :]
        part = jnp.concatenate([part[:, u * unit : (u + 1) * unit] for u in range(UNITS)], axis=0)
        tails.append(jnp.dot(gather, part, preferred_element_type=F32).astype(BF))
    tail = jnp.concatenate(tails, axis=0)
    gate_up = jnp.dot(x_ref[...], w_in_ref[: UNITS * unit, :], preferred_element_type=F32)
    gate_up = gate_up + jnp.dot(tail, w_in_ref[UNITS * unit :, :], preferred_element_type=F32)
    act = (jax.nn.silu(gate_up[:, :hidden]) * gate_up[:, hidden:]).astype(BF)
    y = jnp.dot(act, w_out_ref[...], preferred_element_type=F32)
    for b in range(rows // block):
        part = y[b * block : (b + 1) * block, :]
        moved = jnp.dot(scatter, part[:, UNITS * unit :].astype(BF), preferred_element_type=F32)
        keep = (iota((block, unit), 0) & 7) < CAPE
        for u in range(UNITS):
            out_ref[b * block : (b + 1) * block, u * unit : (u + 1) * unit] = jnp.where(
                keep, part[:, u * unit : (u + 1) * unit], moved[u * block : (u + 1) * block, :]
            ).astype(BF)


def experts(x, w_in, w_out):
    rows, packed = x.shape
    step = 256
    once = pl.Buffered(1)
    return pl.pallas_call(
        experts_kernel,
        grid=(rows // step,),
        out_shape=jax.ShapeDtypeStruct(x.shape, BF),
        in_specs=[
            pl.BlockSpec((step, packed), lambda i: (i, 0)),
            pl.BlockSpec(w_in.shape, lambda i: (0, 0), pipeline_mode=once),
            pl.BlockSpec(w_out.shape, lambda i: (0, 0), pipeline_mode=once),
        ],
        out_specs=pl.BlockSpec((step, packed), lambda i: (i, 0)),
        compiler_params=pltpu.CompilerParams(vmem_limit_bytes=40 << 20),
        cost_estimate=pl.CostEstimate(
            flops=10**10, bytes_accessed=15 * 10**6, transcendentals=10**6
        ),
        name="experts",
    )(x, w_in, w_out)


def combine_kernel(gate_ref, got_ref, out_ref):
    tok = out_ref.shape[0]
    unit = got_ref.shape[1] // UNITS
    tail = jnp.zeros((2 * tok, unit), F32)
    for u in range(UNITS):
        part = got_ref[:, u * unit : (u + 1) * unit]
        main = jnp.dot(gate_ref[0 : 2 * tok, :], part, preferred_element_type=F32)
        out_ref[:, u * unit : (u + 1) * unit] = (main[:tok] + main[tok:]).astype(BF)
        tail = tail + jnp.dot(
            gate_ref[2 * tok * (u + 1) : 2 * tok * (u + 2), :], part, preferred_element_type=F32
        )
    out_ref[:, UNITS * unit :] = (tail[:tok] + tail[tok:]).astype(BF)


def combine(gate, got, tok, width):
    return pl.pallas_call(
        combine_kernel,
        out_shape=jax.ShapeDtypeStruct((tok, width), BF),
        in_specs=[VM, VM],
        out_specs=VM,
        cost_estimate=pl.CostEstimate(flops=10**9, bytes_accessed=4 * 10**6, transcendentals=0),
        name="combine",
    )(gate, got)


def swap(x):
    return lax.all_to_all(x, AXES, split_axis=0, concat_axis=0, tiled=True)


def per_device(tokens, routes, router, w_in, w_out, cache_prefill, page_slot):
    devices = lax.axis_size("row") * lax.axis_size("col")
    pages = page_slot.shape[0]
    slots = lax.all_gather(page_slot, AXES, axis=0, tiled=False)
    first = (lax.axis_index(AXES) * pages).astype(jnp.int32).reshape(1)
    routes_t = routes.T
    arrived = swap(dispatch(routes_t, tokens))
    gate = gates(routes_t, tokens, router.T)
    slot_row = jnp.pad(page_slot, (0, 128 - pages), constant_values=-1)
    slot_row = jnp.tile(slot_row, 8).reshape(1, 1024)
    moved = swap(pages_out(slot_row, cache_prefill, devices))
    returned = swap(experts(arrived, w_in[0], w_out[0]))
    cache_decode = pages_in(first, slots, moved, pages)
    moe_out = combine(gate, returned, tokens.shape[0], tokens.shape[1])
    return (moe_out, cache_decode)


def solution(mesh):
    in_specs = (
        P(AXES, None),
        P(AXES, None),
        P(),
        P(AXES, None, None),
        P(AXES, None, None),
        P(AXES, None),
        P(AXES),
    )
    out_specs = (P(AXES, None), P(AXES, None))
    return jax.shard_map(
        per_device, mesh=mesh, in_specs=in_specs, out_specs=out_specs, check_vma=False
    )
```

time: 214 us -> 209 us (0.977)
  blocking collectives: 0 us -> 93.6 us
  local copies, waits for them, and re-layouts: 73.9 us -> 8.14 us
  Pallas kernels: 0 us -> 33.4 us
  waiting for transfers between devices: 68.9 us -> 50.6 us
  other arithmetic: 17.8 us -> 0 us
  matrix products: 15.7 us -> 0 us
  starting transfers between devices: 34.5 us -> 21.5 us
    unnamed x0 -> x1, blocking collectives: none -> 93.6 us
    pallas_call x0 -> x6, Pallas kernels: none -> 33.4 us  [the longest x1 16.5 us: experts(): pl.pallas_call(experts_kernel, grid=(rows // step,), out_shape=jax.ShapeD...]
    all_to_all x4 -> x3, waiting for transfers between devices: 68.9 us -> 50.6 us  [swap(): return lax.all_to_all(x, AXES, split_axis=0, concat_axis=0, tiled=True)]
    gather x6 -> x0, local copies, waits for them, and re-layouts: 16.5 us -> none  [the longest x1 7.19 us: move_pages(): outgoing = extended[source_of].reshape(devices, page_cap, page_width)]
    dot_general x3 -> x0, matrix products: 15.7 us -> none  [the longest x1 12.5 us: expert_halves(): jnp.einsum('ajcd,jdf->ajcf', buffer, w_in, preferred_element_type=jnp.flo...]
    all_to_all x4 -> x3, starting transfers between devices: 34.5 us -> 21.5 us  [swap(): return lax.all_to_all(x, AXES, split_axis=0, concat_axis=0, tiled=True)]
    unnamed x9 -> x16, local copies, waits for them, and re-layouts: 19.9 us -> 8.04 us
    scatter x4 -> x0, local copies, waits for them, and re-layouts: 10.1 us -> none  [the longest x1 7.32 us: move_pages(): jnp.zeros_like(extended).at[arrived_slot.reshape(-1)]]
  transfers between devices with their start and end apart: 4 -> 3, of which waited for: 3 -> 2; matrix products, arithmetic and copies ran while one was open for 41% -> 0% of each run, Pallas kernels for 0% -> 13%
where the time goes in v1:
time: 209 us; the launch traced here: 208 us
  blocking collectives  93.6 us (45%)
  waiting for transfers between devices  50.6 us (24%)
  Pallas kernels  33.4 us (16%)
  starting transfers between devices  21.5 us (10%)
  local copies, waits for them, and re-layouts  8.14 us (4%)
    unnamed x1, blocking collectives  93.6 us
    all_to_all x3, waiting for transfers between devices, swap(): return lax.all_to_all(x, AXES, split_axis=0, concat_axis=0, tiled=True)  50.6 us
    all_to_all x3, starting transfers between devices, swap(): return lax.all_to_all(x, AXES, split_axis=0, concat_axis=0, tiled=True)  21.5 us
    pallas_call x1, Pallas kernels, experts(): pl.pallas_call(experts_kernel, grid=(rows // step,), out_shape=jax.ShapeD...  16.5 us
    unnamed x16, local copies, waits for them, and re-layouts  8.04 us
    pallas_call x1, Pallas kernels, pages_in(): pl.pallas_call(pages_in_kernel, out_shape=jax.ShapeDtypeStruct((pages, ch...  4.82 us
  transfers between devices with their start and end apart: 3, of which 2 were waited for; matrix products, arithmetic and copies ran while one was open for 0% of the time, Pallas kernels for 13%

profile of v1, /device:TPU:0, one launch (start us, length us, event | category | flops | bytes accessed | tf_op | source)
XLA Modules:
  0.0 208.1 jit_solution(13355781623732511364)
XLA Ops:
  0.6 0.0 copy-start.1
  0.6 0.9 copy-done.1
  1.5 0.0 copy-start.2
  1.5 0.7 copy-done.2
  2.2 2.8 %dispatch.1 = bf16[1024,1536]{1,0:T(8,128)(2,1)} custom-call(s32[6,32]{1,0:T(8,128)S(1)} %bitcast.15, bf16[32,2048]{1,0:T(8,128)(2,1)S(1)} %copy-done.1), custom_call_target="tpu_custom_call" | custom-call | flops 100000000 | bytes 4000000 | tf_op jit(solution)/shard_map/dispatch/pallas_call | solution.py:55
  5.0 0.0 copy-start.6
  5.0 11.1 %all-to-all-start = ((bf16[128,8,1536]{2,1,0:T(8,128)(2,1)}), bf16[128,8,1536]{2,1,0:T(8,128)(2,1)S(1)}, u32[]{:S(2)}, u32[]{:S(2)}) async-start(bf16[128,8,1536]{2,1,0:T(8,128)(2,1)} %bitcast.2), calls=%async_computation | async-start | bytes 6291456 | tf_op jit(solution)/shard_map/all_to_all | solution.py:267
  16.1 0.0 copy-done.6
  16.2 0.0 copy-start.4
  16.2 1.3 copy-done.4
  17.5 3.0 %pages_out.1 = bf16[1024,1152]{1,0:T(8,128)(2,1)S(1)} custom-call(s32[1,1024]{1,0:T(1,128)S(1)} %bitcast.16, bf16[72,9216]{1,0:T(8,128)(2,1)S(1)} %copy-done.4), custom_call_target="tpu_custom_call" | custom-call | flops 2000000000 | bytes 4000000 | tf_op jit(solution)/shard_map/pages_out/pallas_call | solution.py:133
  20.5 0.0 copy-start
  20.5 1.4 copy-done
  21.9 35.9 %all-to-all-done = bf16[128,8,1536]{2,1,0:T(8,128)(2,1)S(1)} async-done(((bf16[128,8,1536]{2,1,0:T(8,128)(2,1)}), bf16[128,8,1536]{2,1,0:T(8,128)(2,1)S(1)}, u32[]{:S(2)}, u32[]{:S(2)}) %all-to-all-start) | async-done | bytes 3145760 | tf_op jit(solution)/shard_map/all_to_all | solution.py:267
  57.9 5.7 %all-to-all-start.2 = ((bf16[128,8,1152]{2,1,0:T(8,128)(2,1)}), bf16[128,8,1152]{2,1,0:T(8,128)(2,1)}, u32[]{:S(2)}, u32[]{:S(2)}) async-start(bf16[128,8,1152]{2,1,0:T(8,128)(2,1)} %bitcast.13), calls=%async_computation.2 | async-start | bytes 4718592 | tf_op jit(solution)/shard_map/all_to_all | solution.py:267
  63.6 0.0 copy-start.3
  63.6 1.8 copy-done.3
  65.4 16.5 %experts.1 = bf16[1024,1536]{1,0:T(8,128)(2,1)} custom-call(bf16[1024,1536]{1,0:T(8,128)(2,1)S(1)} %bitcast.12, bf16[2048,1408]{1,0:T(8,128)(2,1)} %bitcast.20, bf16[704,2048]{1,0:T(8,128)(2,1)S(1)} %bitcast.17), custom_call_target="tpu_custom_call" | custom-call | flops 10000000000 | bytes 15000000 | tf_op jit(solution)/shard_map/experts/pallas_call | solution.py:223
  81.9 14.7 %all-to-all-done.2 = bf16[128,8,1152]{2,1,0:T(8,128)(2,1)} async-done(((bf16[128,8,1152]{2,1,0:T(8,128)(2,1)}), bf16[128,8,1152]{2,1,0:T(8,128)(2,1)}, u32[]{:S(2)}, u32[]{:S(2)}) %all-to-all-start.2) | async-done | bytes 2359328 | tf_op jit(solution)/shard_map/all_to_all | solution.py:267
  96.6 4.7 %all-to-all-start.1 = ((bf16[128,8,1536]{2,1,0:T(8,128)(2,1)}), bf16[128,8,1536]{2,1,0:T(8,128)(2,1)S(1)}, u32[]{:S(2)}, u32[]{:S(2)}) async-start(bf16[128,8,1536]{2,1,0:T(8,128)(2,1)} %bitcast.6), calls=%async_computation.1 | async-start | bytes 6291456 | tf_op jit(solution)/shard_map/all_to_all | solution.py:267
  101.3 0.3 dynamic-update-slice
  101.6 93.6 %all-reduce.1 = s32[9216]{0:T(1024)S(1)} all-reduce(s32[9216]{0:T(1024)S(1)} %dynamic-update-slice), channel_id=2, replica_groups=mesh['row'=8,'col'=16] {'row','col'}, use_global_device_ids=true, to_apply=%add.1 | all-reduce | flops 9216 | bytes 73728
  195.2 0.1 reshape.15.slots_ref
  195.3 2.4 %gates.1.gate_ref = bf16[256,1024]{1,0:T(8,128)(2,1)} custom-call(s32[6,32]{1,0:T(8,128)} %bitcast.14, bf16[32,2048]{1,0:T(8,128)(2,1)} %tok_ref.3, bf16[64,2048]{1,0:T(8,128)(2,1)} %bitcast.19), custom_call_target="tpu_custom_call" | custom-call | flops 100000000 | bytes 2000000 | tf_op jit(solution)/shard_map/gates/pallas_call | solution.py:104
  197.8 4.8 %pages_in.1 = bf16[72,9216]{1,0:T(8,128)(2,1)} custom-call(s32[1]{0:T(128)} %bitcast.8.first_ref, s32[128,72]{1,0:T(8,128)S(1)} %reshape.15.slots_ref, bf16[1024,1152]{1,0:T(8,128)(2,1)} %bitcast.11.got_ref), custom_call_target="tpu_custom_call" | custom-call | flops 2000000000 | bytes 4000000 | tf_op jit(solution)/shard_map/pages_in/pallas_call | solution.py:167
  202.6 0.0 all-to-all-done.1
  202.6 0.0 copy-start.5
  202.6 1.6 copy-done.5
  204.2 3.9 %combine.1 = bf16[32,2048]{1,0:T(8,128)(2,1)} custom-call(bf16[256,1024]{1,0:T(8,128)(2,1)} %gates.1.gate_ref, bf16[1024,1536]{1,0:T(8,128)(2,1)} %bitcast.18), custom_call_target="tpu_custom_call" | custom-call | flops 1000000000 | bytes 4000000 | tf_op jit(solution)/shard_map/combine/pallas_call | solution.py:256
  (3 shorter events, 0.0 us)
Async XLA Ops:
  0.6 0.9 copy-start.1
  1.5 0.7 copy-start.2
  5.0 11.2 %copy-start.6 = (s32[72]{0:T(128)S(1)}, s32[72]{0:T(128)}, u32[]{:S(2)}) copy-start(s32[72]{0:T(128)} %param.13) | copy-start | bytes 868
  5.0 52.9 %all-to-all-start = ((bf16[128,8,1536]{2,1,0:T(8,128)(2,1)}), bf16[128,8,1536]{2,1,0:T(8,128)(2,1)S(1)}, u32[]{:S(2)}, u32[]{:S(2)}) async-start(bf16[128,8,1536]{2,1,0:T(8,128)(2,1)} %bitcast.2), calls=%async_computation | async-start | bytes 6291456 | tf_op jit(solution)/shard_map/all_to_all | solution.py:267
  16.2 1.3 copy-start.4
  20.5 1.4 copy-start
  57.9 38.7 %all-to-all-start.2 = ((bf16[128,8,1152]{2,1,0:T(8,128)(2,1)}), bf16[128,8,1152]{2,1,0:T(8,128)(2,1)}, u32[]{:S(2)}, u32[]{:S(2)}) async-start(bf16[128,8,1152]{2,1,0:T(8,128)(2,1)} %bitcast.13), calls=%async_computation.2 | async-start | bytes 4718592 | tf_op jit(solution)/shard_map/all_to_all | solution.py:267
  63.6 1.8 copy-start.3
  96.6 106.0 %all-to-all-start.1 = ((bf16[128,8,1536]{2,1,0:T(8,128)(2,1)}), bf16[128,8,1536]{2,1,0:T(8,128)(2,1)S(1)}, u32[]{:S(2)}, u32[]{:S(2)}) async-start(bf16[128,8,1536]{2,1,0:T(8,128)(2,1)} %bitcast.6), calls=%async_computation.1 | async-start | bytes 6291456 | tf_op jit(solution)/shard_map/all_to_all | solution.py:267
  202.6 1.6 copy-start.5

commit v2 on v1

--- a/solution.py
+++ b/solution.py
@@ -113,7 +113,8 @@
 
 def pages_out_kernel(slot_ref, cache_ref, out_ref, stack_ref):
     pages, width = cache_ref.shape
-    rows, chunk = out_ref.shape
+    rows = out_ref.shape[0]
+    chunk = width // 8
     for c in range(8):
         stack_ref[c * 128 : c * 128 + pages, :] = cache_ref[:, c * chunk : (c + 1) * chunk]
         stack_ref[c * 128 + pages : (c + 1) * 128, :] = jnp.zeros((128 - pages, chunk), BF)
@@ -125,14 +126,17 @@
         hit = (slot >= first) & (slot < first + pages)
         hit = hit & ((iota((step, 1024), 1) >> 7) == (row & 7))
         got = jnp.dot(onehot(hit), stack_ref[...], preferred_element_type=F32)
-        out_ref[b * step : (b + 1) * step, :] = got.astype(BF)
+        out_ref[b * step : (b + 1) * step, :chunk] = got.astype(BF)
+        landing = jnp.sum(jnp.where(hit, slot - first + 1, 0), axis=1, keepdims=True)
+        landing = jnp.broadcast_to(landing.astype(F32), (step, 128))
+        out_ref[b * step : (b + 1) * step, chunk:] = landing.astype(BF)
 
 
 def pages_out(slot_row, cache, devices):
     width = cache.shape[1]
     return pl.pallas_call(
         pages_out_kernel,
-        out_shape=jax.ShapeDtypeStruct((devices * 8, width // 8), BF),
+        out_shape=jax.ShapeDtypeStruct((devices * 8, width // 8 + 128), BF),
         in_specs=[VM, VM],
         out_specs=VM,
         scratch_shapes=[pltpu.VMEM((1024, width // 8), BF)],
@@ -142,37 +146,36 @@
     )(slot_row, cache)
 
 
-def pages_in_kernel(first_ref, slots_ref, got_ref, out_ref):
+def pages_in_kernel(got_ref, out_ref):
     pages, width = out_ref.shape
-    rows, chunk = got_ref.shape
-    devices = slots_ref.shape[0]
-    local = slots_ref[...] - first_ref[0]
-    hit = (local >= 0) & (local < pages)
-    local = jnp.sum(jnp.where(hit, local + 1, 0), axis=1, keepdims=True).astype(F32)
-    spread = (iota((devices, rows), 1) >> 3) == iota((devices, rows), 0)
-    table = jnp.where(spread, local, 0.0).astype(BF)
-    ones = jnp.ones((8, devices), BF)
-    line = jnp.dot(ones, table, preferred_element_type=F32)[0:1, :].astype(jnp.int32)
+    rows = got_ref.shape[0]
+    chunk = width // 8
+    landing = got_ref[:, chunk : chunk + 128].astype(F32)
+    square = jnp.where(iota((128, 128), 0) == iota((128, 128), 1), 1.0, 0.0)
+    line = [
+        jnp.sum(landing[b * 128 : (b + 1) * 128, :] * square, axis=0, keepdims=True)
+        for b in range(rows // 128)
+    ]
+    line = jnp.concatenate(line, axis=1).astype(jnp.int32)
     pad = -(-pages // 16) * 16
     sub = iota((pad, rows), 1) & 7
     same = line == iota((pad, rows), 0) + 1
     pick = jnp.concatenate([onehot(same & (sub == c)) for c in range(8)], axis=0)
-    placed = jnp.dot(pick, got_ref[...], preferred_element_type=F32)
+    placed = jnp.dot(pick, got_ref[:, :chunk], preferred_element_type=F32)
     for c in range(8):
         out_ref[:, c * chunk : (c + 1) * chunk] = placed[c * pad : c * pad + pages, :].astype(BF)
 
 
-def pages_in(first, slots, got, pages):
-    rows, chunk = got.shape
+def pages_in(got, pages, width):
     return pl.pallas_call(
         pages_in_kernel,
-        out_shape=jax.ShapeDtypeStruct((pages, chunk * 8), BF),
-        in_specs=[pl.BlockSpec(memory_space=pltpu.SMEM), VM, VM],
+        out_shape=jax.ShapeDtypeStruct((pages, width), BF),
+        in_specs=[VM],
         out_specs=VM,
         compiler_params=pltpu.CompilerParams(vmem_limit_bytes=40 << 20),
         cost_estimate=pl.CostEstimate(flops=2 * 10**9, bytes_accessed=4 * 10**6, transcendentals=0),
         name="pages_in",
-    )(first, slots, got)
+    )(got)
 
 
 def experts_kernel(x_ref, w_in_ref, w_out_ref, out_ref):
@@ -270,8 +273,6 @@
 def per_device(tokens, routes, router, w_in, w_out, cache_prefill, page_slot):
     devices = lax.axis_size("row") * lax.axis_size("col")
     pages = page_slot.shape[0]
-    slots = lax.all_gather(page_slot, AXES, axis=0, tiled=False)
-    first = (lax.axis_index(AXES) * pages).astype(jnp.int32).reshape(1)
     routes_t = routes.T
     arrived = swap(dispatch(routes_t, tokens))
     gate = gates(routes_t, tokens, router.T)
@@ -279,7 +280,7 @@
     slot_row = jnp.tile(slot_row, 8).reshape(1, 1024)
     moved = swap(pages_out(slot_row, cache_prefill, devices))
     returned = swap(experts(arrived, w_in[0], w_out[0]))
-    cache_decode = pages_in(first, slots, moved, pages)
+    cache_decode = pages_in(moved, pages, cache_prefill.shape[1])
     moe_out = combine(gate, returned, tokens.shape[0], tokens.shape[1])
     return (moe_out, cache_decode)
 

time: 209 us -> 152 us (0.73)
  blocking collectives: 93.6 us -> 0 us
  waiting for transfers between devices: 50.6 us -> 86.6 us
    unnamed x1 -> x0, blocking collectives: 93.6 us -> none
    all_to_all x3, waiting for transfers between devices: 50.6 us -> 86.6 us  [swap(): return lax.all_to_all(x, AXES, split_axis=0, concat_axis=0, tiled=True)]
  transfers between devices with their start and end apart: 3 -> 3, of which waited for: 2 -> 3; matrix products, arithmetic and copies ran while one was open for 0% -> 0% of each run, Pallas kernels for 13% -> 17%
where the time goes in v2:
time: 152 us; the launch traced here: 151 us
  waiting for transfers between devices  86.6 us (57%)
  Pallas kernels  33 us (22%)
  starting transfers between devices  21.5 us (14%)
  local copies, waits for them, and re-layouts  9.48 us (6%)
    all_to_all x3, waiting for transfers between devices, swap(): return lax.all_to_all(x, AXES, split_axis=0, concat_axis=0, tiled=True)  86.6 us
    all_to_all x3, starting transfers between devices, swap(): return lax.all_to_all(x, AXES, split_axis=0, concat_axis=0, tiled=True)  21.5 us
    pallas_call x1, Pallas kernels, experts(): pl.pallas_call(experts_kernel, grid=(rows // step,), out_shape=jax.ShapeD...  15.6 us
    unnamed x16, local copies, waits for them, and re-layouts  9.48 us
    pallas_call x1, Pallas kernels, pages_in(): pl.pallas_call(pages_in_kernel, out_shape=jax.ShapeDtypeStruct((pages, wi...  4.71 us
    pallas_call x1, Pallas kernels, combine(): pl.pallas_call(combine_kernel, out_shape=jax.ShapeDtypeStruct((tok, width...  3.91 us
    pallas_call x1, Pallas kernels, pages_out(): pl.pallas_call(pages_out_kernel, out_shape=jax.ShapeDtypeStruct((devices...  3.57 us
  transfers between devices with their start and end apart: 3, of which 3 were waited for; matrix products, arithmetic and copies ran while one was open for 0% of the time, Pallas kernels for 17%

profile of v2, /device:TPU:0, one launch (start us, length us, event | category | flops | bytes accessed | tf_op | source)
XLA Modules:
  0.0 151.3 jit_solution(13345178365122188251)
XLA Ops:
  0.6 0.0 copy-start.2
  0.6 0.9 copy-done.2
  1.5 0.0 copy-start.3
  1.5 0.7 copy-done.3
  2.2 2.8 %dispatch.1 = bf16[1024,1536]{1,0:T(8,128)(2,1)} custom-call(s32[6,32]{1,0:T(8,128)S(1)} %bitcast.15, bf16[32,2048]{1,0:T(8,128)(2,1)S(1)} %copy-done.2), custom_call_target="tpu_custom_call" | custom-call | flops 100000000 | bytes 4000000 | tf_op jit(solution)/shard_map/dispatch/pallas_call | solution.py:55
  5.0 0.0 copy-start.7
  5.0 11.1 %all-to-all-start = ((bf16[128,8,1536]{2,1,0:T(8,128)(2,1)}), bf16[128,8,1536]{2,1,0:T(8,128)(2,1)S(1)}, u32[]{:S(2)}, u32[]{:S(2)}) async-start(bf16[128,8,1536]{2,1,0:T(8,128)(2,1)} %bitcast.2), calls=%async_computation | async-start | bytes 6291456 | tf_op jit(solution)/shard_map/all_to_all | solution.py:270
  16.1 0.0 copy-done.7
  16.2 0.0 copy-start.5
  16.2 1.3 copy-done.5
  17.5 3.6 %pages_out.1 = bf16[1024,1280]{1,0:T(8,128)(2,1)S(1)} custom-call(s32[1,1024]{1,0:T(1,128)S(1)} %bitcast.16, bf16[72,9216]{1,0:T(8,128)(2,1)S(1)} %copy-done.5), custom_call_target="tpu_custom_call" | custom-call | flops 2000000000 | bytes 4000000 | tf_op jit(solution)/shard_map/pages_out/pallas_call | solution.py:137
  21.1 0.0 copy-start.1
  21.1 1.5 copy-done.1
  22.6 35.3 %all-to-all-done = bf16[128,8,1536]{2,1,0:T(8,128)(2,1)S(1)} async-done(((bf16[128,8,1536]{2,1,0:T(8,128)(2,1)}), bf16[128,8,1536]{2,1,0:T(8,128)(2,1)S(1)}, u32[]{:S(2)}, u32[]{:S(2)}) %all-to-all-start) | async-done | bytes 3145760 | tf_op jit(solution)/shard_map/all_to_all | solution.py:270
  57.9 5.7 %all-to-all-start.2 = ((bf16[128,8,1280]{2,1,0:T(8,128)(2,1)}), bf16[128,8,1280]{2,1,0:T(8,128)(2,1)}, u32[]{:S(2)}, u32[]{:S(2)}) async-start(bf16[128,8,1280]{2,1,0:T(8,128)(2,1)} %bitcast.13), calls=%async_computation.2 | async-start | bytes 5242880 | tf_op jit(solution)/shard_map/all_to_all | solution.py:270
  63.6 0.0 copy-start.4
  63.6 1.8 %copy-done.4 = bf16[1,704,2048]{2,1,0:T(8,128)(2,1)S(1)} copy-done((bf16[1,704,2048]{2,1,0:T(8,128)(2,1)S(1)}, bf16[1,704,2048]{2,1,0:T(8,128)(2,1)}, u32[]{:S(2)}) %copy-start.4) | copy-done | bytes 2883608
  65.4 15.6 %experts.1 = bf16[1024,1536]{1,0:T(8,128)(2,1)S(1)} custom-call(bf16[1024,1536]{1,0:T(8,128)(2,1)S(1)} %bitcast.11, bf16[2048,1408]{1,0:T(8,128)(2,1)} %bitcast.20, bf16[704,2048]{1,0:T(8,128)(2,1)S(1)} %bitcast.17), custom_call_target="tpu_custom_call" | custom-call | flops 10000000000 | bytes 15000000 | tf_op jit(solution)/shard_map/experts/pallas_call | solution.py:226
  81.0 0.0 copy-start
  81.0 1.6 %copy-done = bf16[1024,1536]{1,0:T(8,128)(2,1)} copy-done((bf16[1024,1536]{1,0:T(8,128)(2,1)}, bf16[1024,1536]{1,0:T(8,128)(2,1)S(1)}, u32[]{:S(2)}) %copy-start) | copy-done | bytes 3145752
  82.6 16.7 %all-to-all-done.2 = bf16[128,8,1280]{2,1,0:T(8,128)(2,1)} async-done(((bf16[128,8,1280]{2,1,0:T(8,128)(2,1)}), bf16[128,8,1280]{2,1,0:T(8,128)(2,1)}, u32[]{:S(2)}, u32[]{:S(2)}) %all-to-all-start.2) | async-done | bytes 2621472 | tf_op jit(solution)/shard_map/all_to_all | solution.py:270
  99.4 4.7 %all-to-all-start.1 = ((bf16[128,8,1536]{2,1,0:T(8,128)(2,1)}), bf16[128,8,1536]{2,1,0:T(8,128)(2,1)S(1)}, u32[]{:S(2)}, u32[]{:S(2)}) async-start(bf16[128,8,1536]{2,1,0:T(8,128)(2,1)} %bitcast.12), calls=%async_computation.1 | async-start | bytes 6291456 | tf_op jit(solution)/shard_map/all_to_all | solution.py:270
  104.1 2.4 %gates.1.gate_ref = bf16[256,1024]{1,0:T(8,128)(2,1)} custom-call(s32[6,32]{1,0:T(8,128)} %bitcast.14, bf16[32,2048]{1,0:T(8,128)(2,1)} %tok_ref.3, bf16[64,2048]{1,0:T(8,128)(2,1)} %bitcast.19), custom_call_target="tpu_custom_call" | custom-call | flops 100000000 | bytes 2000000 | tf_op jit(solution)/shard_map/gates/pallas_call | solution.py:104
  106.5 4.7 %pages_in.1 = bf16[72,9216]{1,0:T(8,128)(2,1)} custom-call(bf16[1024,1280]{1,0:T(8,128)(2,1)} %bitcast.10.got_ref), custom_call_target="tpu_custom_call" | custom-call | flops 2000000000 | bytes 4000000 | tf_op jit(solution)/shard_map/pages_in/pallas_call | solution.py:170
  111.2 34.6 %all-to-all-done.1 = bf16[128,8,1536]{2,1,0:T(8,128)(2,1)S(1)} async-done(((bf16[128,8,1536]{2,1,0:T(8,128)(2,1)}), bf16[128,8,1536]{2,1,0:T(8,128)(2,1)S(1)}, u32[]{:S(2)}, u32[]{:S(2)}) %all-to-all-start.1) | async-done | bytes 3145760 | tf_op jit(solution)/shard_map/all_to_all | solution.py:270
  145.8 0.0 copy-start.6
  145.8 1.6 %copy-done.6 = bf16[128,8,1536]{2,1,0:T(8,128)(2,1)} copy-done((bf16[128,8,1536]{2,1,0:T(8,128)(2,1)}, bf16[128,8,1536]{2,1,0:T(8,128)(2,1)S(1)}, u32[]{:S(2)}) %copy-start.6) | copy-done | bytes 3145752
  147.4 3.9 %combine.1 = bf16[32,2048]{1,0:T(8,128)(2,1)} custom-call(bf16[256,1024]{1,0:T(8,128)(2,1)} %gates.1.gate_ref, bf16[1024,1536]{1,0:T(8,128)(2,1)} %bitcast.18), custom_call_target="tpu_custom_call" | custom-call | flops 1000000000 | bytes 4000000 | tf_op jit(solution)/shard_map/combine/pallas_call | solution.py:259
  (2 shorter events, 0.0 us)
Async XLA Ops:
  0.6 0.9 copy-start.2
  1.5 0.7 copy-start.3
  5.0 11.2 %copy-start.7 = (s32[72]{0:T(128)S(1)}, s32[72]{0:T(128)}, u32[]{:S(2)}) copy-start(s32[72]{0:T(128)} %param.13) | copy-start | bytes 868
  5.0 52.9 %all-to-all-start = ((bf16[128,8,1536]{2,1,0:T(8,128)(2,1)}), bf16[128,8,1536]{2,1,0:T(8,128)(2,1)S(1)}, u32[]{:S(2)}, u32[]{:S(2)}) async-start(bf16[128,8,1536]{2,1,0:T(8,128)(2,1)} %bitcast.2), calls=%async_computation | async-start | bytes 6291456 | tf_op jit(solution)/shard_map/all_to_all | solution.py:270
  16.2 1.3 copy-start.5
  21.1 1.5 copy-start.1
  57.9 41.5 %all-to-all-start.2 = ((bf16[128,8,1280]{2,1,0:T(8,128)(2,1)}), bf16[128,8,1280]{2,1,0:T(8,128)(2,1)}, u32[]{:S(2)}, u32[]{:S(2)}) async-start(bf16[128,8,1280]{2,1,0:T(8,128)(2,1)} %bitcast.13), calls=%async_computation.2 | async-start | bytes 5242880 | tf_op jit(solution)/shard_map/all_to_all | solution.py:270
  63.6 1.8 %copy-start.4 = (bf16[1,704,2048]{2,1,0:T(8,128)(2,1)S(1)}, bf16[1,704,2048]{2,1,0:T(8,128)(2,1)}, u32[]{:S(2)}) copy-start(bf16[1,704,2048]{2,1,0:T(8,128)(2,1)} %param.11) | copy-start | bytes 8650756
  81.0 1.6 %copy-start = (bf16[1024,1536]{1,0:T(8,128)(2,1)}, bf16[1024,1536]{1,0:T(8,128)(2,1)S(1)}, u32[]{:S(2)}) copy-start(bf16[1024,1536]{1,0:T(8,128)(2,1)S(1)} %experts.1) | copy-start | bytes 9437188
  99.4 46.4 %all-to-all-start.1 = ((bf16[128,8,1536]{2,1,0:T(8,128)(2,1)}), bf16[128,8,1536]{2,1,0:T(8,128)(2,1)S(1)}, u32[]{:S(2)}, u32[]{:S(2)}) async-start(bf16[128,8,1536]{2,1,0:T(8,128)(2,1)} %bitcast.12), calls=%async_computation.1 | async-start | bytes 6291456 | tf_op jit(solution)/shard_map/all_to_all | solution.py:270
  145.8 1.6 %copy-start.6 = (bf16[128,8,1536]{2,1,0:T(8,128)(2,1)}, bf16[128,8,1536]{2,1,0:T(8,128)(2,1)S(1)}, u32[]{:S(2)}) copy-start(bf16[128,8,1536]{2,1,0:T(8,128)(2,1)S(1)} %all-to-all-done.1) | copy-start | bytes 9437188

commit v3 on v2

--- a/solution.py
+++ b/solution.py
@@ -9,8 +9,10 @@
 
 EXPERTS = 64
 CAPE = 6
+CHUNKS = 2
 ROUTE_SCALE = 2.446
 AXES = ("row", "col")
+SWAP = ("col", "row")
 BF = jnp.bfloat16
 F32 = jnp.float32
 VM = pl.BlockSpec(memory_space=pltpu.VMEM)
@@ -27,12 +29,21 @@
     return jnp.where(cond, 1.0, 0.0).astype(BF)
 
 
-def dispatch_kernel(routes_ref, tok_ref, out_ref):
+def expert_of(message):
+    return ((message & 3) << 4) + (message >> 3)
+
+
+def dispatch_kernel(routes_hbm, tok_hbm, out_hbm, routes_ref, tok_ref, buf_ref, in_sem, out_sem):
     tok = tok_ref.shape[0]
-    rows = out_ref.shape[0] // 2
-    unit = out_ref.shape[1] // UNITS
+    rows = EXPERTS * 8
+    unit = buf_ref.shape[3]
+    load_routes = pltpu.make_async_copy(routes_hbm, routes_ref, in_sem.at[0])
+    load_tok = pltpu.make_async_copy(tok_hbm, tok_ref, in_sem.at[1])
+    load_routes.start()
+    load_tok.start()
+    load_routes.wait()
     row = iota((rows, tok), 0)
-    expert, sub = row >> 3, row & 7
+    expert, sub = expert_of(((row >> 5) << 3) + ((row >> 3) & 3)), row & 7
     named = routes_ref[0:1, :] == expert
     for k in range(1, routes_ref.shape[0]):
         named = named | (routes_ref[k : k + 1, :] == expert)
@@ -40,27 +51,46 @@
     rank = jnp.dot(onehot(named), before, preferred_element_type=F32).astype(jnp.int32)
     rank = jnp.where(named, rank, 99)
     main = onehot(rank == sub)
+    load_tok.wait()
     last = tok_ref[:, UNITS * unit :]
+    stores = []
     for u in range(UNITS):
         tail = onehot((sub >= CAPE) & (rank == sub + (2 * u - CAPE)))
         picked = jnp.dot(main, tok_ref[:, u * unit : (u + 1) * unit], preferred_element_type=F32)
         picked = picked + jnp.dot(tail, last, preferred_element_type=F32)
-        picked = picked.astype(BF)
-        out_ref[0:rows, u * unit : (u + 1) * unit] = picked
-        out_ref[rows : 2 * rows, u * unit : (u + 1) * unit] = picked
+        buf_ref[u] = picked.astype(BF).reshape(buf_ref.shape[1:])
+        for half in range(2):
+            store = pltpu.make_async_copy(
+                buf_ref.at[u],
+                out_hbm.at[:, half, :, u * unit : (u + 1) * unit],
+                out_sem.at[2 * u + half],
+            )
+            store.start()
+            stores.append(store)
+    for store in stores:
+        store.wait()
 
 
 def dispatch(routes_t, tokens):
     width = tokens.shape[1]
-    return pl.pallas_call(
+    unit = width * CAPE // 8 // UNITS
+    hbm = pl.BlockSpec(memory_space=pltpu.HBM)
+    out = pl.pallas_call(
         dispatch_kernel,
-        out_shape=jax.ShapeDtypeStruct((2 * EXPERTS * 8, width * CAPE // 8), BF),
-        in_specs=[VM, VM],
-        out_specs=VM,
-        compiler_params=pltpu.CompilerParams(vmem_limit_bytes=24 << 20),
+        out_shape=jax.ShapeDtypeStruct((16, 2, 32, UNITS * unit), BF),
+        in_specs=[hbm, hbm],
+        out_specs=hbm,
+        scratch_shapes=[
+            pltpu.VMEM(routes_t.shape, jnp.int32),
+            pltpu.VMEM(tokens.shape, BF),
+            pltpu.VMEM((UNITS, 16, 32, unit), BF),
+            pltpu.SemaphoreType.DMA((2,)),
+            pltpu.SemaphoreType.DMA((2 * UNITS,)),
+        ],
         cost_estimate=pl.CostEstimate(flops=10**8, bytes_accessed=4 * 10**6, transcendentals=0),
         name="dispatch",
     )(routes_t, tokens)
+    return out.reshape(2 * EXPERTS * 8, UNITS * unit)
 
 
 def gates_kernel(routes_ref, tok_ref, router_ref, out_ref):
@@ -85,7 +115,7 @@
     gate = ROUTE_SCALE * picked / jnp.sum(picked, axis=1, keepdims=True)
     high = gate.astype(BF)
     low = (gate - high.astype(F32)).astype(BF)
-    spread = onehot(((iota((EXPERTS, cols), 1) >> 3) & (EXPERTS - 1)) == iota((EXPERTS, cols), 0))
+    spread = onehot(expert_of(iota((EXPERTS, cols), 1) >> 3) == iota((EXPERTS, cols), 0))
     rank = jnp.dot(rank.astype(BF), spread, preferred_element_type=F32).astype(jnp.int32)
     high = jnp.dot(high, spread, preferred_element_type=F32)
     low = jnp.dot(low, spread, preferred_element_type=F32)
@@ -106,40 +136,38 @@
         out_shape=jax.ShapeDtypeStruct((2 * (UNITS + 1) * tok, 2 * EXPERTS * 8), BF),
         in_specs=[VM, VM, VM],
         out_specs=VM,
+        compiler_params=pltpu.CompilerParams(vmem_limit_bytes=16 << 20),
         cost_estimate=pl.CostEstimate(flops=10**8, bytes_accessed=2 * 10**6, transcendentals=0),
         name="gates",
     )(routes_t, tokens, router_t)
 
 
-def pages_out_kernel(slot_ref, cache_ref, out_ref, stack_ref):
+def pages_out_kernel(slot_ref, cache_ref, out_ref):
     pages, width = cache_ref.shape
-    rows = out_ref.shape[0]
-    chunk = width // 8
-    for c in range(8):
-        stack_ref[c * 128 : c * 128 + pages, :] = cache_ref[:, c * chunk : (c + 1) * chunk]
-        stack_ref[c * 128 + pages : (c + 1) * 128, :] = jnp.zeros((128 - pages, chunk), BF)
-    step = 256
-    for b in range(rows // step):
-        row = iota((step, 1024), 0) + b * step
-        first = (row >> 3) * pages
-        slot = slot_ref[...]
-        hit = (slot >= first) & (slot < first + pages)
-        hit = hit & ((iota((step, 1024), 1) >> 7) == (row & 7))
-        got = jnp.dot(onehot(hit), stack_ref[...], preferred_element_type=F32)
-        out_ref[b * step : (b + 1) * step, :chunk] = got.astype(BF)
-        landing = jnp.sum(jnp.where(hit, slot - first + 1, 0), axis=1, keepdims=True)
-        landing = jnp.broadcast_to(landing.astype(F32), (step, 128))
-        out_ref[b * step : (b + 1) * step, chunk:] = landing.astype(BF)
+    devices, chunks, _ = out_ref.shape
+    chunk = width // chunks
+    message = iota((devices, pages), 0)
+    first = ((message & 7) * 16 + (message >> 3)) * pages
+    slot = slot_ref[...]
+    hit = (slot >= first) & (slot < first + pages)
+    landing = jnp.sum(jnp.where(hit, slot - first + 1, 0), axis=1, keepdims=True)
+    landing = jnp.broadcast_to(landing.astype(F32), (devices, 128))
+    pick = onehot(hit)
+    for c in range(chunks):
+        got = jnp.dot(
+            pick, cache_ref[:, c * chunk : (c + 1) * chunk], preferred_element_type=F32
+        )
+        out_ref[:, c, :chunk] = got.astype(BF)
+        out_ref[:, c, chunk:] = landing.astype(BF)
 
 
 def pages_out(slot_row, cache, devices):
     width = cache.shape[1]
     return pl.pallas_call(
         pages_out_kernel,
-        out_shape=jax.ShapeDtypeStruct((devices * 8, width // 8 + 128), BF),
+        out_shape=jax.ShapeDtypeStruct((devices, CHUNKS, width // CHUNKS + 128), BF),
         in_specs=[VM, VM],
         out_specs=VM,
-        scratch_shapes=[pltpu.VMEM((1024, width // 8), BF)],
         compiler_params=pltpu.CompilerParams(vmem_limit_bytes=40 << 20),
         cost_estimate=pl.CostEstimate(flops=2 * 10**9, bytes_accessed=4 * 10**6, transcendentals=0),
         name="pages_out",
@@ -148,22 +176,15 @@
 
 def pages_in_kernel(got_ref, out_ref):
     pages, width = out_ref.shape
-    rows = got_ref.shape[0]
-    chunk = width // 8
-    landing = got_ref[:, chunk : chunk + 128].astype(F32)
-    square = jnp.where(iota((128, 128), 0) == iota((128, 128), 1), 1.0, 0.0)
-    line = [
-        jnp.sum(landing[b * 128 : (b + 1) * 128, :] * square, axis=0, keepdims=True)
-        for b in range(rows // 128)
-    ]
-    line = jnp.concatenate(line, axis=1).astype(jnp.int32)
-    pad = -(-pages // 16) * 16
-    sub = iota((pad, rows), 1) & 7
-    same = line == iota((pad, rows), 0) + 1
-    pick = jnp.concatenate([onehot(same & (sub == c)) for c in range(8)], axis=0)
-    placed = jnp.dot(pick, got_ref[:, :chunk], preferred_element_type=F32)
-    for c in range(8):
-        out_ref[:, c * chunk : (c + 1) * chunk] = placed[c * pad : c * pad + pages, :].astype(BF)
+    devices, chunks, _ = got_ref.shape
+    chunk = width // chunks
+    landing = got_ref[:, 0, chunk:].astype(F32)
+    square = jnp.where(iota((devices, 128), 0) == iota((devices, 128), 1), 1.0, 0.0)
+    line = jnp.sum(landing * square, axis=0, keepdims=True).astype(jnp.int32)
+    pick = onehot(line == iota((pages, devices), 0) + 1)
+    for c in range(chunks):
+        placed = jnp.dot(pick, got_ref[:, c, :chunk], preferred_element_type=F32)
+        out_ref[:, c * chunk : (c + 1) * chunk] = placed.astype(BF)
 
 
 def pages_in(got, pages, width):
@@ -172,7 +193,7 @@
         out_shape=jax.ShapeDtypeStruct((pages, width), BF),
         in_specs=[VM],
         out_specs=VM,
-        compiler_params=pltpu.CompilerParams(vmem_limit_bytes=40 << 20),
+        compiler_params=pltpu.CompilerParams(vmem_limit_bytes=16 << 20),
         cost_estimate=pl.CostEstimate(flops=2 * 10**9, bytes_accessed=4 * 10**6, transcendentals=0),
         name="pages_in",
     )(got)
@@ -241,33 +262,80 @@
     )(x, w_in, w_out)
 
 
-def combine_kernel(gate_ref, got_ref, out_ref):
+def combine_kernel(gate_hbm, got_ref, out_ref, total_ref, gate_ref, sem):
     tok = out_ref.shape[0]
     unit = got_ref.shape[1] // UNITS
+    step = pl.program_id(0)
+    steps = gate_ref.shape[0]
+    block = gate_ref.shape[2]
+
+    def load(i):
+        return pltpu.make_async_copy(
+            gate_hbm.at[:, i * block : (i + 1) * block], gate_ref.at[i], sem.at[i]
+        )
+
+    @pl.when(step == 0)
+    def _():
+        for i in range(steps):
+            load(i).start()
+
+    for i in range(steps):
+
+        @pl.when(step == i)
+        def _():
+            load(i).wait()
+
+    gate = gate_ref[step]
+    parts = []
     tail = jnp.zeros((2 * tok, unit), F32)
     for u in range(UNITS):
         part = got_ref[:, u * unit : (u + 1) * unit]
-        main = jnp.dot(gate_ref[0 : 2 * tok, :], part, preferred_element_type=F32)
-        out_ref[:, u * unit : (u + 1) * unit] = (main[:tok] + main[tok:]).astype(BF)
+        parts.append(jnp.dot(gate[0 : 2 * tok, :], part, preferred_element_type=F32))
         tail = tail + jnp.dot(
-            gate_ref[2 * tok * (u + 1) : 2 * tok * (u + 2), :], part, preferred_element_type=F32
+            gate[2 * tok * (u + 1) : 2 * tok * (u + 2), :], part, preferred_element_type=F32
         )
-    out_ref[:, UNITS * unit :] = (tail[:tok] + tail[tok:]).astype(BF)
+    parts.append(tail)
+
+    @pl.when(step == 0)
+    def _():
+        for u in range(UNITS + 1):
+            total_ref[:, u * unit : (u + 1) * unit] = parts[u]
+
+    @pl.when(step > 0)
+    def _():
+        for u in range(UNITS + 1):
+            total_ref[:, u * unit : (u + 1) * unit] += parts[u]
+
+    @pl.when(step == pl.num_programs(0) - 1)
+    def _():
+        out_ref[...] = (total_ref[:tok, :] + total_ref[tok:, :]).astype(BF)
 
 
 def combine(gate, got, tok, width):
+    rows, packed = got.shape
+    step = 256
     return pl.pallas_call(
         combine_kernel,
+        grid=(rows // step,),
         out_shape=jax.ShapeDtypeStruct((tok, width), BF),
-        in_specs=[VM, VM],
-        out_specs=VM,
+        in_specs=[
+            pl.BlockSpec(memory_space=pltpu.HBM),
+            pl.BlockSpec((step, packed), lambda i: (i, 0)),
+        ],
+        out_specs=pl.BlockSpec((tok, width), lambda i: (0, 0)),
+        scratch_shapes=[
+            pltpu.VMEM((2 * tok, width), F32),
+            pltpu.VMEM((rows // step, gate.shape[0], step), BF),
+            pltpu.SemaphoreType.DMA((rows // step,)),
+        ],
+        compiler_params=pltpu.CompilerParams(vmem_limit_bytes=12 << 20),
         cost_estimate=pl.CostEstimate(flops=10**9, bytes_accessed=4 * 10**6, transcendentals=0),
         name="combine",
     )(gate, got)
 
 
 def swap(x):
-    return lax.all_to_all(x, AXES, split_axis=0, concat_axis=0, tiled=True)
+    return lax.all_to_all(x, SWAP, split_axis=0, concat_axis=0, tiled=True)
 
 
 def per_device(tokens, routes, router, w_in, w_out, cache_prefill, page_slot):
@@ -276,9 +344,7 @@
     routes_t = routes.T
     arrived = swap(dispatch(routes_t, tokens))
     gate = gates(routes_t, tokens, router.T)
-    slot_row = jnp.pad(page_slot, (0, 128 - pages), constant_values=-1)
-    slot_row = jnp.tile(slot_row, 8).reshape(1, 1024)
-    moved = swap(pages_out(slot_row, cache_prefill, devices))
+    moved = swap(pages_out(page_slot.reshape(1, pages), cache_prefill, devices))
     returned = swap(experts(arrived, w_in[0], w_out[0]))
     cache_decode = pages_in(moved, pages, cache_prefill.shape[1])
     moe_out = combine(gate, returned, tokens.shape[0], tokens.shape[1])

time: 152 us -> 143 us (0.941)
  waiting for transfers between devices: 86.6 us -> 78.9 us
    all_to_all x3, waiting for transfers between devices: 86.6 us -> 78.9 us  [swap(): return lax.all_to_all(x, SWAP, split_axis=0, concat_axis=0, tiled=True)]
    pallas_call x1, Pallas kernels: 4.71 us -> 8.55 us  [pages_in(): pl.pallas_call(pages_in_kernel, out_shape=jax.ShapeDtypeStruct((pages, wi...]
    pallas_call x3, Pallas kernels: 10.2 us -> 7.22 us  [the longest x1 3.24 us: dispatch(): pl.pallas_call(dispatch_kernel, out_shape=jax.ShapeDtypeStruct((16, 2, 32...]
    pallas_call x1, Pallas kernels: 2.44 us -> 0.6 us  [gates(): pl.pallas_call(gates_kernel, out_shape=jax.ShapeDtypeStruct((2 * (UNITS +...]
    unnamed x16 -> x20, local copies, waits for them, and re-layouts: 9.48 us -> 8.02 us
  transfers between devices with their start and end apart: 3 -> 3, of which waited for: 3 -> 3; matrix products, arithmetic and copies ran while one was open for 0% -> 0% of each run, Pallas kernels for 17% -> 18%
where the time goes in v3:
time: 143 us; the launch traced here: 142 us
  waiting for transfers between devices  78.9 us (55%)
  Pallas kernels  31.9 us (22%)
  starting transfers between devices  22.6 us (16%)
  local copies, waits for them, and re-layouts  8.02 us (6%)
    all_to_all x3, waiting for transfers between devices, swap(): return lax.all_to_all(x, SWAP, split_axis=0, concat_axis=0, tiled=True)  78.9 us
    all_to_all x3, starting transfers between devices, swap(): return lax.all_to_all(x, SWAP, split_axis=0, concat_axis=0, tiled=True)  22.6 us
    pallas_call x1, Pallas kernels, experts(): pl.pallas_call(experts_kernel, grid=(rows // step,), out_shape=jax.ShapeD...  15.6 us
    pallas_call x1, Pallas kernels, pages_in(): pl.pallas_call(pages_in_kernel, out_shape=jax.ShapeDtypeStruct((pages, wi...  8.55 us
    unnamed x20, local copies, waits for them, and re-layouts  8.02 us
    pallas_call x1, Pallas kernels, dispatch(): pl.pallas_call(dispatch_kernel, out_shape=jax.ShapeDtypeStruct((16, 2, 32...  3.24 us
  transfers between devices with their start and end apart: 3, of which 3 were waited for; matrix products, arithmetic and copies ran while one was open for 0% of the time, Pallas kernels for 18%

profile of v3, /device:TPU:0, one launch (start us, length us, event | category | flops | bytes accessed | tf_op | source)
XLA Modules:
  0.0 142.4 jit_solution(3178198382035901641)
XLA Ops:
  0.6 3.2 %dispatch.1 = bf16[16,2,32,1536]{3,2,1,0:T(8,128)(2,1)} custom-call(s32[6,32]{1,0:T(8,128)} %bitcast.13, bf16[32,2048]{1,0:T(8,128)(2,1)} %tok_hbm.1), custom_call_target="tpu_custom_call" | custom-call | flops 100000000 | bytes 4000000 | tf_op jit(solution)/shard_map/dispatch/pallas_call | solution.py:78
  3.9 0.0 copy-start.9
  3.9 11.1 %all-to-all-start = ((bf16[128,8,1536]{2,1,0:T(8,128)(2,1)}), bf16[128,8,1536]{2,1,0:T(8,128)(2,1)S(1)}, u32[]{:S(2)}, u32[]{:S(2)}) async-start(bf16[128,8,1536]{2,1,0:T(8,128)(2,1)} %bitcast.17), calls=%async_computation | async-start | bytes 6291456 | tf_op jit(solution)/shard_map/all_to_all | solution.py:338
  15.0 0.0 copy-done.9
  15.1 0.0 copy-start.8
  15.1 1.3 copy-done.8
  16.4 1.4 pages_out.1
  17.8 0.0 copy-start.1
  17.8 1.4 copy-done.1
  19.2 36.0 %all-to-all-done = bf16[128,8,1536]{2,1,0:T(8,128)(2,1)S(1)} async-done(((bf16[128,8,1536]{2,1,0:T(8,128)(2,1)}), bf16[128,8,1536]{2,1,0:T(8,128)(2,1)S(1)}, u32[]{:S(2)}, u32[]{:S(2)}) %all-to-all-start) | async-done | bytes 3145760 | tf_op jit(solution)/shard_map/all_to_all | solution.py:338
  55.2 5.8 %all-to-all-start.2 = ((bf16[128,2,4736]{2,1,0:T(2,128)(2,1)}), bf16[128,2,4736]{2,1,0:T(2,128)(2,1)}, u32[]{:S(2)}, u32[]{:S(2)}) async-start(bf16[128,2,4736]{2,1,0:T(2,128)(2,1)} %copy-done.1), calls=%async_computation.2 | async-start | bytes 4849664 | tf_op jit(solution)/shard_map/all_to_all | solution.py:338
  61.0 0.0 copy-start.7
  61.0 1.8 %copy-done.7 = bf16[1,704,2048]{2,1,0:T(8,128)(2,1)S(1)} copy-done((bf16[1,704,2048]{2,1,0:T(8,128)(2,1)S(1)}, bf16[1,704,2048]{2,1,0:T(8,128)(2,1)}, u32[]{:S(2)}) %copy-start.7) | copy-done | bytes 2883608
  62.9 15.6 %experts.1 = bf16[1024,1536]{1,0:T(8,128)(2,1)S(1)} custom-call(bf16[1024,1536]{1,0:T(8,128)(2,1)S(1)} %bitcast.10, bf16[2048,1408]{1,0:T(8,128)(2,1)} %bitcast.18, bf16[704,2048]{1,0:T(8,128)(2,1)S(1)} %bitcast.15), custom_call_target="tpu_custom_call" | custom-call | flops 10000000000 | bytes 15000000 | tf_op jit(solution)/shard_map/experts/pallas_call | solution.py:247
  78.4 0.0 copy-start
  78.5 1.6 %copy-done = bf16[1024,1536]{1,0:T(8,128)(2,1)} copy-done((bf16[1024,1536]{1,0:T(8,128)(2,1)}, bf16[1024,1536]{1,0:T(8,128)(2,1)S(1)}, u32[]{:S(2)}) %copy-start) | copy-done | bytes 3145752
  80.1 13.0 %all-to-all-done.2.got_ref = bf16[128,2,4736]{2,1,0:T(2,128)(2,1)} async-done(((bf16[128,2,4736]{2,1,0:T(2,128)(2,1)}), bf16[128,2,4736]{2,1,0:T(2,128)(2,1)}, u32[]{:S(2)}, u32[]{:S(2)}) %all-to-all-start.2) | async-done | bytes 2424864 | tf_op jit(solution)/shard_map/all_to_all | solution.py:338
  93.1 0.0 copy-start.4
  93.1 0.0 copy-start.5
  93.1 0.0 copy-start.6
  93.1 5.6 %all-to-all-start.1 = ((bf16[128,8,1536]{2,1,0:T(8,128)(2,1)}), bf16[128,8,1536]{2,1,0:T(8,128)(2,1)S(1)}, u32[]{:S(2)}, u32[]{:S(2)}) async-start(bf16[128,8,1536]{2,1,0:T(8,128)(2,1)} %bitcast.11), calls=%async_computation.1 | async-start | bytes 6291456 | tf_op jit(solution)/shard_map/all_to_all | solution.py:338
  98.7 0.0 copy-done.4
  98.7 0.0 copy-done.5
  98.7 0.0 copy-done.6
  98.7 0.6 gates.1.gate_hbm
  99.3 0.0 copy-start.2
  99.3 0.8 copy-done.2
  100.1 8.6 %pages_in.1 = bf16[72,9216]{1,0:T(8,128)(2,1)} custom-call(bf16[128,2,4736]{2,1,0:T(2,128)(2,1)} %all-to-all-done.2.got_ref), custom_call_target="tpu_custom_call" | custom-call | flops 2000000000 | bytes 4000000 | tf_op jit(solution)/shard_map/pages_in/pallas_call | solution.py:191
  108.7 30.0 %all-to-all-done.1 = bf16[128,8,1536]{2,1,0:T(8,128)(2,1)S(1)} async-done(((bf16[128,8,1536]{2,1,0:T(8,128)(2,1)}), bf16[128,8,1536]{2,1,0:T(8,128)(2,1)S(1)}, u32[]{:S(2)}, u32[]{:S(2)}) %all-to-all-start.1) | async-done | bytes 3145760 | tf_op jit(solution)/shard_map/all_to_all | solution.py:338
  138.7 0.0 copy-start.3
  138.7 1.0 copy-done.3
  139.7 2.6 %combine.1 = bf16[32,2048]{1,0:T(8,128)(2,1)} custom-call(bf16[256,1024]{1,0:T(8,128)(2,1)S(1)} %copy-done.3, bf16[1024,1536]{1,0:T(8,128)(2,1)S(1)} %bitcast.9), custom_call_target="tpu_custom_call" | custom-call | flops 1000000000 | bytes 4000000 | tf_op jit(solution)/shard_map/combine/pallas_call | solution.py:317
Async XLA Ops:
  3.9 11.2 %copy-start.9 = (s32[72]{0:T(128)S(1)}, s32[72]{0:T(128)}, u32[]{:S(2)}) copy-start(s32[72]{0:T(128)} %param.13) | copy-start | bytes 868
  3.9 51.3 %all-to-all-start = ((bf16[128,8,1536]{2,1,0:T(8,128)(2,1)}), bf16[128,8,1536]{2,1,0:T(8,128)(2,1)S(1)}, u32[]{:S(2)}, u32[]{:S(2)}) async-start(bf16[128,8,1536]{2,1,0:T(8,128)(2,1)} %bitcast.17), calls=%async_computation | async-start | bytes 6291456 | tf_op jit(solution)/shard_map/all_to_all | solution.py:338
  15.1 1.3 copy-start.8
  17.8 1.4 %copy-start.1 = (bf16[128,2,4736]{2,1,0:T(2,128)(2,1)}, bf16[128,2,4736]{2,1,0:T(2,128)(2,1)S(1)}, u32[]{:S(2)}) copy-start(bf16[128,2,4736]{2,1,0:T(2,128)(2,1)S(1)} %pages_out.1) | copy-start | bytes 7274500
  55.2 37.9 %all-to-all-start.2 = ((bf16[128,2,4736]{2,1,0:T(2,128)(2,1)}), bf16[128,2,4736]{2,1,0:T(2,128)(2,1)}, u32[]{:S(2)}, u32[]{:S(2)}) async-start(bf16[128,2,4736]{2,1,0:T(2,128)(2,1)} %copy-done.1), calls=%async_computation.2 | async-start | bytes 4849664 | tf_op jit(solution)/shard_map/all_to_all | solution.py:338
  61.0 1.8 %copy-start.7 = (bf16[1,704,2048]{2,1,0:T(8,128)(2,1)S(1)}, bf16[1,704,2048]{2,1,0:T(8,128)(2,1)}, u32[]{:S(2)}) copy-start(bf16[1,704,2048]{2,1,0:T(8,128)(2,1)} %param.11) | copy-start | bytes 8650756
  78.4 1.6 %copy-start = (bf16[1024,1536]{1,0:T(8,128)(2,1)}, bf16[1024,1536]{1,0:T(8,128)(2,1)S(1)}, u32[]{:S(2)}) copy-start(bf16[1024,1536]{1,0:T(8,128)(2,1)S(1)} %experts.1) | copy-start | bytes 9437188
  93.1 5.6 %copy-start.4 = (bf16[32,2048]{1,0:T(8,128)(2,1)S(1)}, bf16[32,2048]{1,0:T(8,128)(2,1)}, u32[]{:S(2)}) copy-start(bf16[32,2048]{1,0:T(8,128)(2,1)} %tok_hbm.1) | copy-start | bytes 393220
  93.1 5.6 %copy-start.5 = (bf16[2048,64]{0,1:T(8,128)(2,1)S(1)}, bf16[2048,64]{0,1:T(8,128)(2,1)}, u32[]{:S(2)}) copy-start(bf16[2048,64]{0,1:T(8,128)(2,1)} %param.9) | copy-start | bytes 786436
  93.1 5.6 %copy-start.6 = (s32[32,6]{0,1:T(8,128)S(1)}, s32[32,6]{0,1:T(8,128)}, u32[]{:S(2)}) copy-start(s32[32,6]{0,1:T(8,128)} %param.8) | copy-start | bytes 2308
  93.1 45.6 %all-to-all-start.1 = ((bf16[128,8,1536]{2,1,0:T(8,128)(2,1)}), bf16[128,8,1536]{2,1,0:T(8,128)(2,1)S(1)}, u32[]{:S(2)}, u32[]{:S(2)}) async-start(bf16[128,8,1536]{2,1,0:T(8,128)(2,1)} %bitcast.11), calls=%async_computation.1 | async-start | bytes 6291456 | tf_op jit(solution)/shard_map/all_to_all | solution.py:338
  99.3 0.8 copy-start.2
  138.7 1.0 copy-start.3

commit v4 on v3

--- a/solution.py
+++ b/solution.py
@@ -42,22 +42,23 @@
     load_routes.start()
     load_tok.start()
     load_routes.wait()
-    row = iota((rows, tok), 0)
+    row, col = iota((rows, 2 * tok), 0), iota((rows, 2 * tok), 1)
     expert, sub = expert_of(((row >> 5) << 3) + ((row >> 3) & 3)), row & 7
-    named = routes_ref[0:1, :] == expert
+    routes = jnp.concatenate([routes_ref[...], routes_ref[...]], axis=1)
+    named = routes[0:1, :] == expert
     for k in range(1, routes_ref.shape[0]):
-        named = named | (routes_ref[k : k + 1, :] == expert)
-    before = onehot(iota((tok, tok), 0) < iota((tok, tok), 1))
+        named = named | (routes[k : k + 1, :] == expert)
+    first, second = iota((2 * tok, 2 * tok), 0), iota((2 * tok, 2 * tok), 1)
+    before = onehot(first < jnp.where(second < tok, second, second - tok))
     rank = jnp.dot(onehot(named), before, preferred_element_type=F32).astype(jnp.int32)
     rank = jnp.where(named, rank, 99)
-    main = onehot(rank == sub)
     load_tok.wait()
     last = tok_ref[:, UNITS * unit :]
     stores = []
     for u in range(UNITS):
-        tail = onehot((sub >= CAPE) & (rank == sub + (2 * u - CAPE)))
-        picked = jnp.dot(main, tok_ref[:, u * unit : (u + 1) * unit], preferred_element_type=F32)
-        picked = picked + jnp.dot(tail, last, preferred_element_type=F32)
+        wanted = jnp.where(col < tok, sub, jnp.where(sub >= CAPE, sub + (2 * u - CAPE), -1))
+        source = jnp.concatenate([tok_ref[:, u * unit : (u + 1) * unit], last], axis=0)
+        picked = jnp.dot(onehot(rank == wanted), source, preferred_element_type=F32)
         buf_ref[u] = picked.astype(BF).reshape(buf_ref.shape[1:])
         for half in range(2):
             store = pltpu.make_async_copy(
@@ -262,76 +263,49 @@
     )(x, w_in, w_out)
 
 
-def combine_kernel(gate_hbm, got_ref, out_ref, total_ref, gate_ref, sem):
+def combine_kernel(gate_hbm, got_ref, out_ref, gate_ref, sem):
     tok = out_ref.shape[0]
     unit = got_ref.shape[1] // UNITS
-    step = pl.program_id(0)
-    steps = gate_ref.shape[0]
-    block = gate_ref.shape[2]
-
-    def load(i):
-        return pltpu.make_async_copy(
+    blocks, _, block = gate_ref.shape
+    loads = []
+    for i in range(blocks):
+        load = pltpu.make_async_copy(
             gate_hbm.at[:, i * block : (i + 1) * block], gate_ref.at[i], sem.at[i]
         )
-
-    @pl.when(step == 0)
-    def _():
-        for i in range(steps):
-            load(i).start()
-
-    for i in range(steps):
-
-        @pl.when(step == i)
-        def _():
-            load(i).wait()
-
-    gate = gate_ref[step]
-    parts = []
-    tail = jnp.zeros((2 * tok, unit), F32)
-    for u in range(UNITS):
-        part = got_ref[:, u * unit : (u + 1) * unit]
-        parts.append(jnp.dot(gate[0 : 2 * tok, :], part, preferred_element_type=F32))
-        tail = tail + jnp.dot(
-            gate[2 * tok * (u + 1) : 2 * tok * (u + 2), :], part, preferred_element_type=F32
-        )
-    parts.append(tail)
-
-    @pl.when(step == 0)
-    def _():
-        for u in range(UNITS + 1):
-            total_ref[:, u * unit : (u + 1) * unit] = parts[u]
-
-    @pl.when(step > 0)
-    def _():
-        for u in range(UNITS + 1):
-            total_ref[:, u * unit : (u + 1) * unit] += parts[u]
-
-    @pl.when(step == pl.num_programs(0) - 1)
-    def _():
-        out_ref[...] = (total_ref[:tok, :] + total_ref[tok:, :]).astype(BF)
+        load.start()
+        loads.append(load)
+    total = [jnp.zeros((2 * tok, unit), F32) for _ in range(UNITS + 1)]
+    for i in range(blocks):
+        loads[i].wait()
+        for u in range(UNITS):
+            part = got_ref[i * block : (i + 1) * block, u * unit : (u + 1) * unit]
+            main = gate_ref[i, 0 : 2 * tok, :]
+            tail = gate_ref[i, 2 * tok * (u + 1) : 2 * tok * (u + 2), :]
+            both = jnp.dot(
+                jnp.concatenate([main, tail], axis=0), part, preferred_element_type=F32
+            )
+            total[u] = total[u] + both[: 2 * tok]
+            total[UNITS] = total[UNITS] + both[2 * tok :]
+    for u in range(UNITS + 1):
+        out_ref[:, u * unit : (u + 1) * unit] = (total[u][:tok] + total[u][tok:]).astype(BF)
 
 
 def combine(gate, got, tok, width):
-    rows, packed = got.shape
-    step = 256
+    rows = got.shape[0]
+    block = 256
     return pl.pallas_call(
         combine_kernel,
-        grid=(rows // step,),
         out_shape=jax.ShapeDtypeStruct((tok, width), BF),
-        in_specs=[
-            pl.BlockSpec(memory_space=pltpu.HBM),
-            pl.BlockSpec((step, packed), lambda i: (i, 0)),
-        ],
-        out_specs=pl.BlockSpec((tok, width), lambda i: (0, 0)),
+        in_specs=[pl.BlockSpec(memory_space=pltpu.HBM), VM],
+        out_specs=VM,
         scratch_shapes=[
-            pltpu.VMEM((2 * tok, width), F32),
-            pltpu.VMEM((rows // step, gate.shape[0], step), BF),
-            pltpu.SemaphoreType.DMA((rows // step,)),
+            pltpu.VMEM((rows // block, gate.shape[0], block), BF),
+            pltpu.SemaphoreType.DMA((rows // block,)),
         ],
         compiler_params=pltpu.CompilerParams(vmem_limit_bytes=12 << 20),
         cost_estimate=pl.CostEstimate(flops=10**9, bytes_accessed=4 * 10**6, transcendentals=0),
         name="combine",
-    )(gate, got)
+    )(pltpu.with_memory_space_constraint(gate, pltpu.HBM), got)
 
 
 def swap(x):

time: 143 us -> 142 us (level)
    unnamed x20 -> x18, local copies, waits for them, and re-layouts: 8.02 us -> 6.99 us
  transfers between devices with their start and end apart: 3 -> 3, of which waited for: 3 -> 3; matrix products, arithmetic and copies ran while one was open for 0% -> 0% of each run, Pallas kernels for 18% -> 19%
where the time goes in v4:
time: 142 us; the launch traced here: 141 us
  waiting for transfers between devices  78.9 us (56%)
  Pallas kernels  31.7 us (22%)
  starting transfers between devices  22.6 us (16%)
  local copies, waits for them, and re-layouts  6.99 us (5%)
    all_to_all x3, waiting for transfers between devices, swap(): return lax.all_to_all(x, SWAP, split_axis=0, concat_axis=0, tiled=True)  78.9 us
    all_to_all x3, starting transfers between devices, swap(): return lax.all_to_all(x, SWAP, split_axis=0, concat_axis=0, tiled=True)  22.6 us
    pallas_call x1, Pallas kernels, experts(): pl.pallas_call(experts_kernel, grid=(rows // step,), out_shape=jax.ShapeD...  15.6 us
    pallas_call x1, Pallas kernels, pages_in(): pl.pallas_call(pages_in_kernel, out_shape=jax.ShapeDtypeStruct((pages, wi...  8.55 us
    unnamed x18, local copies, waits for them, and re-layouts  6.99 us
    pallas_call x1, Pallas kernels, dispatch(): pl.pallas_call(dispatch_kernel, out_shape=jax.ShapeDtypeStruct((16, 2, 32...  3.15 us
  transfers between devices with their start and end apart: 3, of which 3 were waited for; matrix products, arithmetic and copies ran while one was open for 0% of the time, Pallas kernels for 19%

profile of v4, /device:TPU:0, one launch (start us, length us, event | category | flops | bytes accessed | tf_op | source)
XLA Modules:
  0.0 141.1 jit_solution(10785528885699748283)
XLA Ops:
  0.6 3.1 %dispatch.1 = bf16[16,2,32,1536]{3,2,1,0:T(8,128)(2,1)} custom-call(s32[6,32]{1,0:T(8,128)} %bitcast.13, bf16[32,2048]{1,0:T(8,128)(2,1)} %tok_hbm.1), custom_call_target="tpu_custom_call" | custom-call | flops 100000000 | bytes 4000000 | tf_op jit(solution)/shard_map/dispatch/pallas_call | solution.py:79
  3.8 0.0 copy-start.8
  3.8 11.2 %all-to-all-start = ((bf16[128,8,1536]{2,1,0:T(8,128)(2,1)}), bf16[128,8,1536]{2,1,0:T(8,128)(2,1)S(1)}, u32[]{:S(2)}, u32[]{:S(2)}) async-start(bf16[128,8,1536]{2,1,0:T(8,128)(2,1)} %bitcast.17), calls=%async_computation | async-start | bytes 6291456 | tf_op jit(solution)/shard_map/all_to_all | solution.py:312
  15.0 0.0 copy-done.8
  15.0 0.0 copy-start.7
  15.0 1.3 copy-done.7
  16.3 1.4 %pages_out.1 = bf16[128,2,4736]{2,1,0:T(2,128)(2,1)S(1)} custom-call(s32[1,72]{1,0:T(1,128)S(1)} %bitcast.16, bf16[72,9216]{1,0:T(8,128)(2,1)S(1)} %copy-done.7), custom_call_target="tpu_custom_call" | custom-call | flops 2000000000 | bytes 4000000 | tf_op jit(solution)/shard_map/pages_out/pallas_call | solution.py:167
  17.7 0.0 copy-start.1
  17.7 1.4 %copy-done.1 = bf16[128,2,4736]{2,1,0:T(2,128)(2,1)} copy-done((bf16[128,2,4736]{2,1,0:T(2,128)(2,1)}, bf16[128,2,4736]{2,1,0:T(2,128)(2,1)S(1)}, u32[]{:S(2)}) %copy-start.1) | copy-done | bytes 2424856
  19.2 35.9 %all-to-all-done = bf16[128,8,1536]{2,1,0:T(8,128)(2,1)S(1)} async-done(((bf16[128,8,1536]{2,1,0:T(8,128)(2,1)}), bf16[128,8,1536]{2,1,0:T(8,128)(2,1)S(1)}, u32[]{:S(2)}, u32[]{:S(2)}) %all-to-all-start) | async-done | bytes 3145760 | tf_op jit(solution)/shard_map/all_to_all | solution.py:312
  55.1 5.8 %all-to-all-start.2 = ((bf16[128,2,4736]{2,1,0:T(2,128)(2,1)}), bf16[128,2,4736]{2,1,0:T(2,128)(2,1)}, u32[]{:S(2)}, u32[]{:S(2)}) async-start(bf16[128,2,4736]{2,1,0:T(2,128)(2,1)} %copy-done.1), calls=%async_computation.2 | async-start | bytes 4849664 | tf_op jit(solution)/shard_map/all_to_all | solution.py:312
  60.9 0.0 copy-start.6
  61.0 1.8 %copy-done.6 = bf16[1,704,2048]{2,1,0:T(8,128)(2,1)S(1)} copy-done((bf16[1,704,2048]{2,1,0:T(8,128)(2,1)S(1)}, bf16[1,704,2048]{2,1,0:T(8,128)(2,1)}, u32[]{:S(2)}) %copy-start.6) | copy-done | bytes 2883608
  62.8 15.6 %experts.1 = bf16[1024,1536]{1,0:T(8,128)(2,1)S(1)} custom-call(bf16[1024,1536]{1,0:T(8,128)(2,1)S(1)} %bitcast.10, bf16[2048,1408]{1,0:T(8,128)(2,1)} %bitcast.18, bf16[704,2048]{1,0:T(8,128)(2,1)S(1)} %bitcast.15), custom_call_target="tpu_custom_call" | custom-call | flops 10000000000 | bytes 15000000 | tf_op jit(solution)/shard_map/experts/pallas_call | solution.py:248
  78.4 0.0 copy-start
  78.4 1.6 %copy-done = bf16[1024,1536]{1,0:T(8,128)(2,1)} copy-done((bf16[1024,1536]{1,0:T(8,128)(2,1)}, bf16[1024,1536]{1,0:T(8,128)(2,1)S(1)}, u32[]{:S(2)}) %copy-start) | copy-done | bytes 3145752
  80.0 13.0 %all-to-all-done.2.got_ref = bf16[128,2,4736]{2,1,0:T(2,128)(2,1)} async-done(((bf16[128,2,4736]{2,1,0:T(2,128)(2,1)}), bf16[128,2,4736]{2,1,0:T(2,128)(2,1)}, u32[]{:S(2)}, u32[]{:S(2)}) %all-to-all-start.2) | async-done | bytes 2424864 | tf_op jit(solution)/shard_map/all_to_all | solution.py:312
  93.0 0.0 copy-start.3
  93.0 0.0 copy-start.4
  93.0 0.0 copy-start.5
  93.0 5.6 %all-to-all-start.1 = ((bf16[128,8,1536]{2,1,0:T(8,128)(2,1)}), bf16[128,8,1536]{2,1,0:T(8,128)(2,1)S(1)}, u32[]{:S(2)}, u32[]{:S(2)}) async-start(bf16[128,8,1536]{2,1,0:T(8,128)(2,1)} %bitcast.11), calls=%async_computation.1 | async-start | bytes 6291456 | tf_op jit(solution)/shard_map/all_to_all | solution.py:312
  98.6 0.0 copy-done.3
  98.6 0.0 copy-done.4
  98.6 0.0 copy-done.5
  98.6 0.6 gates.1.gate_hbm
  99.2 0.0 copy-start.2
  99.3 0.8 copy-done.2
  100.0 8.6 %pages_in.1 = bf16[72,9216]{1,0:T(8,128)(2,1)} custom-call(bf16[128,2,4736]{2,1,0:T(2,128)(2,1)} %all-to-all-done.2.got_ref), custom_call_target="tpu_custom_call" | custom-call | flops 2000000000 | bytes 4000000 | tf_op jit(solution)/shard_map/pages_in/pallas_call | solution.py:192
  108.6 30.0 %all-to-all-done.1 = bf16[128,8,1536]{2,1,0:T(8,128)(2,1)S(1)} async-done(((bf16[128,8,1536]{2,1,0:T(8,128)(2,1)}), bf16[128,8,1536]{2,1,0:T(8,128)(2,1)S(1)}, u32[]{:S(2)}, u32[]{:S(2)}) %all-to-all-start.1) | async-done | bytes 3145760 | tf_op jit(solution)/shard_map/all_to_all | solution.py:312
  138.6 2.4 %combine.1 = bf16[32,2048]{1,0:T(8,128)(2,1)} custom-call(bf16[256,1024]{1,0:T(8,128)(2,1)} %copy-done.2, bf16[1024,1536]{1,0:T(8,128)(2,1)S(1)} %bitcast.9), custom_call_target="tpu_custom_call" | custom-call | flops 1000000000 | bytes 4000000 | tf_op jit(solution)/shard_map/combine/pallas_call | solution.py:296
Async XLA Ops:
  3.8 11.2 %copy-start.8 = (s32[72]{0:T(128)S(1)}, s32[72]{0:T(128)}, u32[]{:S(2)}) copy-start(s32[72]{0:T(128)} %param.13) | copy-start | bytes 868
  3.8 51.3 %all-to-all-start = ((bf16[128,8,1536]{2,1,0:T(8,128)(2,1)}), bf16[128,8,1536]{2,1,0:T(8,128)(2,1)S(1)}, u32[]{:S(2)}, u32[]{:S(2)}) async-start(bf16[128,8,1536]{2,1,0:T(8,128)(2,1)} %bitcast.17), calls=%async_computation | async-start | bytes 6291456 | tf_op jit(solution)/shard_map/all_to_all | solution.py:312
  15.0 1.3 copy-start.7
  17.7 1.4 %copy-start.1 = (bf16[128,2,4736]{2,1,0:T(2,128)(2,1)}, bf16[128,2,4736]{2,1,0:T(2,128)(2,1)S(1)}, u32[]{:S(2)}) copy-start(bf16[128,2,4736]{2,1,0:T(2,128)(2,1)S(1)} %pages_out.1) | copy-start | bytes 7274500
  55.1 37.9 %all-to-all-start.2 = ((bf16[128,2,4736]{2,1,0:T(2,128)(2,1)}), bf16[128,2,4736]{2,1,0:T(2,128)(2,1)}, u32[]{:S(2)}, u32[]{:S(2)}) async-start(bf16[128,2,4736]{2,1,0:T(2,128)(2,1)} %copy-done.1), calls=%async_computation.2 | async-start | bytes 4849664 | tf_op jit(solution)/shard_map/all_to_all | solution.py:312
  60.9 1.8 %copy-start.6 = (bf16[1,704,2048]{2,1,0:T(8,128)(2,1)S(1)}, bf16[1,704,2048]{2,1,0:T(8,128)(2,1)}, u32[]{:S(2)}) copy-start(bf16[1,704,2048]{2,1,0:T(8,128)(2,1)} %param.11) | copy-start | bytes 8650756
  78.4 1.6 %copy-start = (bf16[1024,1536]{1,0:T(8,128)(2,1)}, bf16[1024,1536]{1,0:T(8,128)(2,1)S(1)}, u32[]{:S(2)}) copy-start(bf16[1024,1536]{1,0:T(8,128)(2,1)S(1)} %experts.1) | copy-start | bytes 9437188
  93.0 5.6 %copy-start.3 = (bf16[32,2048]{1,0:T(8,128)(2,1)S(1)}, bf16[32,2048]{1,0:T(8,128)(2,1)}, u32[]{:S(2)}) copy-start(bf16[32,2048]{1,0:T(8,128)(2,1)} %tok_hbm.1) | copy-start | bytes 393220
  93.0 5.6 %copy-start.4 = (bf16[2048,64]{0,1:T(8,128)(2,1)S(1)}, bf16[2048,64]{0,1:T(8,128)(2,1)}, u32[]{:S(2)}) copy-start(bf16[2048,64]{0,1:T(8,128)(2,1)} %param.9) | copy-start | bytes 786436
  93.0 5.6 %copy-start.5 = (s32[32,6]{0,1:T(8,128)S(1)}, s32[32,6]{0,1:T(8,128)}, u32[]{:S(2)}) copy-start(s32[32,6]{0,1:T(8,128)} %param.8) | copy-start | bytes 2308
  93.0 45.6 %all-to-all-start.1 = ((bf16[128,8,1536]{2,1,0:T(8,128)(2,1)}), bf16[128,8,1536]{2,1,0:T(8,128)(2,1)S(1)}, u32[]{:S(2)}, u32[]{:S(2)}) async-start(bf16[128,8,1536]{2,1,0:T(8,128)(2,1)} %bitcast.11), calls=%async_computation.1 | async-start | bytes 6291456 | tf_op jit(solution)/shard_map/all_to_all | solution.py:312
  99.2 0.8 copy-start.2

commit v5 on v4

--- a/solution.py
+++ b/solution.py
@@ -29,8 +29,8 @@
     return jnp.where(cond, 1.0, 0.0).astype(BF)
 
 
-def expert_of(message):
-    return ((message & 3) << 4) + (message >> 3)
+def slot_expert(row):
+    return (((row >> 3) & 3) << 4) + (row >> 5)
 
 
 def dispatch_kernel(routes_hbm, tok_hbm, out_hbm, routes_ref, tok_ref, buf_ref, in_sem, out_sem):
@@ -43,7 +43,7 @@
     load_tok.start()
     load_routes.wait()
     row, col = iota((rows, 2 * tok), 0), iota((rows, 2 * tok), 1)
-    expert, sub = expert_of(((row >> 5) << 3) + ((row >> 3) & 3)), row & 7
+    expert, sub = slot_expert(row), row & 7
     routes = jnp.concatenate([routes_ref[...], routes_ref[...]], axis=1)
     named = routes[0:1, :] == expert
     for k in range(1, routes_ref.shape[0]):
@@ -116,7 +116,7 @@
     gate = ROUTE_SCALE * picked / jnp.sum(picked, axis=1, keepdims=True)
     high = gate.astype(BF)
     low = (gate - high.astype(F32)).astype(BF)
-    spread = onehot(expert_of(iota((EXPERTS, cols), 1) >> 3) == iota((EXPERTS, cols), 0))
+    spread = onehot(slot_expert(iota((EXPERTS, cols), 1)) == iota((EXPERTS, cols), 0))
     rank = jnp.dot(rank.astype(BF), spread, preferred_element_type=F32).astype(jnp.int32)
     high = jnp.dot(high, spread, preferred_element_type=F32)
     low = jnp.dot(low, spread, preferred_element_type=F32)
@@ -134,7 +134,7 @@
     tok = tokens.shape[0]
     return pl.pallas_call(
         gates_kernel,
-        out_shape=jax.ShapeDtypeStruct((2 * (UNITS + 1) * tok, 2 * EXPERTS * 8), BF),
+        out_shape=jax.ShapeDtypeStruct((2 * (UNITS + 1) * tok, EXPERTS * 8), BF),
         in_specs=[VM, VM, VM],
         out_specs=VM,
         compiler_params=pltpu.CompilerParams(vmem_limit_bytes=16 << 20),
@@ -263,49 +263,44 @@
     )(x, w_in, w_out)
 
 
-def combine_kernel(gate_hbm, got_ref, out_ref, gate_ref, sem):
+def combine_kernel(gate_hbm, got_ref, out_ref, sum_ref, gate_ref, sem):
     tok = out_ref.shape[0]
-    unit = got_ref.shape[1] // UNITS
-    blocks, _, block = gate_ref.shape
-    loads = []
-    for i in range(blocks):
-        load = pltpu.make_async_copy(
-            gate_hbm.at[:, i * block : (i + 1) * block], gate_ref.at[i], sem.at[i]
+    unit = got_ref.shape[2] // UNITS
+    load = pltpu.make_async_copy(gate_hbm, gate_ref, sem)
+    load.start()
+    sums = got_ref[:, :32, :].astype(F32) + got_ref[:, 32:, :].astype(F32)
+    sum_ref[...] = sums.astype(BF).reshape(sum_ref.shape)
+    load.wait()
+    main = gate_ref[0 : 2 * tok, :]
+    total = jnp.zeros((2 * tok, unit), F32)
+    for u in range(UNITS):
+        tail = gate_ref[2 * tok * (u + 1) : 2 * tok * (u + 2), :]
+        both = jnp.dot(
+            jnp.concatenate([main, tail], axis=0),
+            sum_ref[:, u * unit : (u + 1) * unit],
+            preferred_element_type=F32,
         )
-        load.start()
-        loads.append(load)
-    total = [jnp.zeros((2 * tok, unit), F32) for _ in range(UNITS + 1)]
-    for i in range(blocks):
-        loads[i].wait()
-        for u in range(UNITS):
-            part = got_ref[i * block : (i + 1) * block, u * unit : (u + 1) * unit]
-            main = gate_ref[i, 0 : 2 * tok, :]
-            tail = gate_ref[i, 2 * tok * (u + 1) : 2 * tok * (u + 2), :]
-            both = jnp.dot(
-                jnp.concatenate([main, tail], axis=0), part, preferred_element_type=F32
-            )
-            total[u] = total[u] + both[: 2 * tok]
-            total[UNITS] = total[UNITS] + both[2 * tok :]
-    for u in range(UNITS + 1):
-        out_ref[:, u * unit : (u + 1) * unit] = (total[u][:tok] + total[u][tok:]).astype(BF)
+        out_ref[:, u * unit : (u + 1) * unit] = (both[:tok] + both[tok : 2 * tok]).astype(BF)
+        total = total + both[2 * tok :]
+    out_ref[:, UNITS * unit :] = (total[:tok] + total[tok:]).astype(BF)
 
 
 def combine(gate, got, tok, width):
-    rows = got.shape[0]
-    block = 256
+    rows, packed = got.shape
     return pl.pallas_call(
         combine_kernel,
         out_shape=jax.ShapeDtypeStruct((tok, width), BF),
         in_specs=[pl.BlockSpec(memory_space=pltpu.HBM), VM],
         out_specs=VM,
         scratch_shapes=[
-            pltpu.VMEM((rows // block, gate.shape[0], block), BF),
-            pltpu.SemaphoreType.DMA((rows // block,)),
+            pltpu.VMEM((rows // 2, packed), BF),
+            pltpu.VMEM(gate.shape, BF),
+            pltpu.SemaphoreType.DMA,
         ],
         compiler_params=pltpu.CompilerParams(vmem_limit_bytes=12 << 20),
         cost_estimate=pl.CostEstimate(flops=10**9, bytes_accessed=4 * 10**6, transcendentals=0),
         name="combine",
-    )(pltpu.with_memory_space_constraint(gate, pltpu.HBM), got)
+    )(pltpu.with_memory_space_constraint(gate, pltpu.HBM), got.reshape(16, 64, packed))
 
 
 def swap(x):

time: 142 us -> 141 us (level)
  no operation moved by 1% of the time
where the time goes in v5:
time: 141 us
  waiting for transfers between devices  79.1 us (56%)
  Pallas kernels  31.2 us (22%)
  starting transfers between devices  22.6 us (16%)
  local copies, waits for them, and re-layouts  6.9 us (5%)
    all_to_all x3, waiting for transfers between devices, swap(): return lax.all_to_all(x, SWAP, split_axis=0, concat_axis=0, tiled=True)  79.1 us
    all_to_all x3, starting transfers between devices, swap(): return lax.all_to_all(x, SWAP, split_axis=0, concat_axis=0, tiled=True)  22.6 us
    pallas_call x1, Pallas kernels, experts(): pl.pallas_call(experts_kernel, grid=(rows // step,), out_shape=jax.ShapeD...  15.6 us
    pallas_call x1, Pallas kernels, pages_in(): pl.pallas_call(pages_in_kernel, out_shape=jax.ShapeDtypeStruct((pages, wi...  8.55 us
    unnamed x18, local copies, waits for them, and re-layouts  6.9 us
    pallas_call x1, Pallas kernels, dispatch(): pl.pallas_call(dispatch_kernel, out_shape=jax.ShapeDtypeStruct((16, 2, 32...  3.14 us
  transfers between devices with their start and end apart: 3, of which 3 were waited for; matrix products, arithmetic and copies ran while one was open for 0% of the time, Pallas kernels for 19%

profile of v5, /device:TPU:0, one launch (start us, length us, event | category | flops | bytes accessed | tf_op | source)
XLA Modules:
  0.0 140.7 jit_solution(10236298272523201786)
XLA Ops:
  0.6 3.1 %dispatch.1 = bf16[16,2,32,1536]{3,2,1,0:T(8,128)(2,1)} custom-call(s32[6,32]{1,0:T(8,128)} %bitcast.13, bf16[32,2048]{1,0:T(8,128)(2,1)} %tok_hbm.1), custom_call_target="tpu_custom_call" | custom-call | flops 100000000 | bytes 4000000 | tf_op jit(solution)/shard_map/dispatch/pallas_call | solution.py:79
  3.8 0.0 copy-start.8
  3.8 11.2 %all-to-all-start = ((bf16[128,8,1536]{2,1,0:T(8,128)(2,1)}), bf16[128,8,1536]{2,1,0:T(8,128)(2,1)S(1)}, u32[]{:S(2)}, u32[]{:S(2)}) async-start(bf16[128,8,1536]{2,1,0:T(8,128)(2,1)} %bitcast.17), calls=%async_computation | async-start | bytes 6291456 | tf_op jit(solution)/shard_map/all_to_all | solution.py:307
  14.9 0.0 copy-done.8
  15.0 0.0 copy-start.7
  15.0 1.3 copy-done.7
  16.3 1.4 %pages_out.1 = bf16[128,2,4736]{2,1,0:T(2,128)(2,1)S(1)} custom-call(s32[1,72]{1,0:T(1,128)S(1)} %bitcast.16, bf16[72,9216]{1,0:T(8,128)(2,1)S(1)} %copy-done.7), custom_call_target="tpu_custom_call" | custom-call | flops 2000000000 | bytes 4000000 | tf_op jit(solution)/shard_map/pages_out/pallas_call | solution.py:167
  17.7 0.0 copy-start.1
  17.7 1.4 %copy-done.1 = bf16[128,2,4736]{2,1,0:T(2,128)(2,1)} copy-done((bf16[128,2,4736]{2,1,0:T(2,128)(2,1)}, bf16[128,2,4736]{2,1,0:T(2,128)(2,1)S(1)}, u32[]{:S(2)}) %copy-start.1) | copy-done | bytes 2424856
  19.2 35.9 %all-to-all-done = bf16[128,8,1536]{2,1,0:T(8,128)(2,1)S(1)} async-done(((bf16[128,8,1536]{2,1,0:T(8,128)(2,1)}), bf16[128,8,1536]{2,1,0:T(8,128)(2,1)S(1)}, u32[]{:S(2)}, u32[]{:S(2)}) %all-to-all-start) | async-done | bytes 3145760 | tf_op jit(solution)/shard_map/all_to_all | solution.py:307
  55.1 5.8 %all-to-all-start.2 = ((bf16[128,2,4736]{2,1,0:T(2,128)(2,1)}), bf16[128,2,4736]{2,1,0:T(2,128)(2,1)}, u32[]{:S(2)}, u32[]{:S(2)}) async-start(bf16[128,2,4736]{2,1,0:T(2,128)(2,1)} %copy-done.1), calls=%async_computation.2 | async-start | bytes 4849664 | tf_op jit(solution)/shard_map/all_to_all | solution.py:307
  60.9 0.0 copy-start.6
  60.9 1.8 %copy-done.6 = bf16[1,704,2048]{2,1,0:T(8,128)(2,1)S(1)} copy-done((bf16[1,704,2048]{2,1,0:T(8,128)(2,1)S(1)}, bf16[1,704,2048]{2,1,0:T(8,128)(2,1)}, u32[]{:S(2)}) %copy-start.6) | copy-done | bytes 2883608
  62.8 15.6 %experts.1 = bf16[1024,1536]{1,0:T(8,128)(2,1)S(1)} custom-call(bf16[1024,1536]{1,0:T(8,128)(2,1)S(1)} %bitcast.9, bf16[2048,1408]{1,0:T(8,128)(2,1)} %bitcast.18, bf16[704,2048]{1,0:T(8,128)(2,1)S(1)} %bitcast.15), custom_call_target="tpu_custom_call" | custom-call | flops 10000000000 | bytes 15000000 | tf_op jit(solution)/shard_map/experts/pallas_call | solution.py:248
  78.3 0.0 copy-start
  78.4 1.6 %copy-done = bf16[1024,1536]{1,0:T(8,128)(2,1)} copy-done((bf16[1024,1536]{1,0:T(8,128)(2,1)}, bf16[1024,1536]{1,0:T(8,128)(2,1)S(1)}, u32[]{:S(2)}) %copy-start) | copy-done | bytes 3145752
  80.0 13.0 %all-to-all-done.2.got_ref = bf16[128,2,4736]{2,1,0:T(2,128)(2,1)} async-done(((bf16[128,2,4736]{2,1,0:T(2,128)(2,1)}), bf16[128,2,4736]{2,1,0:T(2,128)(2,1)}, u32[]{:S(2)}, u32[]{:S(2)}) %all-to-all-start.2) | async-done | bytes 2424864 | tf_op jit(solution)/shard_map/all_to_all | solution.py:307
  93.0 0.0 copy-start.2
  93.0 0.0 copy-start.3
  93.0 0.0 copy-start.5
  93.0 5.6 %all-to-all-start.1 = ((bf16[128,8,1536]{2,1,0:T(8,128)(2,1)}), bf16[128,8,1536]{2,1,0:T(8,128)(2,1)S(1)}, u32[]{:S(2)}, u32[]{:S(2)}) async-start(bf16[128,8,1536]{2,1,0:T(8,128)(2,1)} %bitcast.10), calls=%async_computation.1 | async-start | bytes 6291456 | tf_op jit(solution)/shard_map/all_to_all | solution.py:307
  98.6 0.0 copy-done.2
  98.6 0.0 copy-done.3
  98.6 0.0 copy-done.5
  98.6 0.5 gates.1.gate_hbm
  99.1 0.0 copy-start.4
  99.1 0.7 copy-done.4
  99.8 8.6 %pages_in.1 = bf16[72,9216]{1,0:T(8,128)(2,1)} custom-call(bf16[128,2,4736]{2,1,0:T(2,128)(2,1)} %all-to-all-done.2.got_ref), custom_call_target="tpu_custom_call" | custom-call | flops 2000000000 | bytes 4000000 | tf_op jit(solution)/shard_map/pages_in/pallas_call | solution.py:192
  108.4 30.2 %all-to-all-done.1 = bf16[128,8,1536]{2,1,0:T(8,128)(2,1)S(1)} async-done(((bf16[128,8,1536]{2,1,0:T(8,128)(2,1)}), bf16[128,8,1536]{2,1,0:T(8,128)(2,1)S(1)}, u32[]{:S(2)}, u32[]{:S(2)}) %all-to-all-start.1) | async-done | bytes 3145760 | tf_op jit(solution)/shard_map/all_to_all | solution.py:307
  138.6 2.0 %combine.1 = bf16[32,2048]{1,0:T(8,128)(2,1)} custom-call(bf16[256,512]{1,0:T(8,128)(2,1)} %copy-done.4, bf16[16,64,1536]{2,1,0:T(8,128)(2,1)S(1)} %bitcast.11), custom_call_target="tpu_custom_call" | custom-call | flops 1000000000 | bytes 4000000 | tf_op jit(solution)/shard_map/combine/pallas_call | solution.py:290
Async XLA Ops:
  3.8 11.2 %copy-start.8 = (s32[72]{0:T(128)S(1)}, s32[72]{0:T(128)}, u32[]{:S(2)}) copy-start(s32[72]{0:T(128)} %param.13) | copy-start | bytes 868
  3.8 51.3 %all-to-all-start = ((bf16[128,8,1536]{2,1,0:T(8,128)(2,1)}), bf16[128,8,1536]{2,1,0:T(8,128)(2,1)S(1)}, u32[]{:S(2)}, u32[]{:S(2)}) async-start(bf16[128,8,1536]{2,1,0:T(8,128)(2,1)} %bitcast.17), calls=%async_computation | async-start | bytes 6291456 | tf_op jit(solution)/shard_map/all_to_all | solution.py:307
  15.0 1.3 copy-start.7
  17.7 1.4 %copy-start.1 = (bf16[128,2,4736]{2,1,0:T(2,128)(2,1)}, bf16[128,2,4736]{2,1,0:T(2,128)(2,1)S(1)}, u32[]{:S(2)}) copy-start(bf16[128,2,4736]{2,1,0:T(2,128)(2,1)S(1)} %pages_out.1) | copy-start | bytes 7274500
  55.1 37.9 %all-to-all-start.2 = ((bf16[128,2,4736]{2,1,0:T(2,128)(2,1)}), bf16[128,2,4736]{2,1,0:T(2,128)(2,1)}, u32[]{:S(2)}, u32[]{:S(2)}) async-start(bf16[128,2,4736]{2,1,0:T(2,128)(2,1)} %copy-done.1), calls=%async_computation.2 | async-start | bytes 4849664 | tf_op jit(solution)/shard_map/all_to_all | solution.py:307
  60.9 1.8 %copy-start.6 = (bf16[1,704,2048]{2,1,0:T(8,128)(2,1)S(1)}, bf16[1,704,2048]{2,1,0:T(8,128)(2,1)}, u32[]{:S(2)}) copy-start(bf16[1,704,2048]{2,1,0:T(8,128)(2,1)} %param.11) | copy-start | bytes 8650756
  78.3 1.6 %copy-start = (bf16[1024,1536]{1,0:T(8,128)(2,1)}, bf16[1024,1536]{1,0:T(8,128)(2,1)S(1)}, u32[]{:S(2)}) copy-start(bf16[1024,1536]{1,0:T(8,128)(2,1)S(1)} %experts.1) | copy-start | bytes 9437188
  93.0 5.6 %copy-start.2 = (bf16[32,2048]{1,0:T(8,128)(2,1)S(1)}, bf16[32,2048]{1,0:T(8,128)(2,1)}, u32[]{:S(2)}) copy-start(bf16[32,2048]{1,0:T(8,128)(2,1)} %tok_hbm.1) | copy-start | bytes 393220
  93.0 5.6 %copy-start.3 = (bf16[2048,64]{0,1:T(8,128)(2,1)S(1)}, bf16[2048,64]{0,1:T(8,128)(2,1)}, u32[]{:S(2)}) copy-start(bf16[2048,64]{0,1:T(8,128)(2,1)} %param.9) | copy-start | bytes 786436
  93.0 5.6 %copy-start.5 = (s32[32,6]{0,1:T(8,128)S(1)}, s32[32,6]{0,1:T(8,128)}, u32[]{:S(2)}) copy-start(s32[32,6]{0,1:T(8,128)} %param.8) | copy-start | bytes 2308
  93.0 45.6 %all-to-all-start.1 = ((bf16[128,8,1536]{2,1,0:T(8,128)(2,1)}), bf16[128,8,1536]{2,1,0:T(8,128)(2,1)S(1)}, u32[]{:S(2)}, u32[]{:S(2)}) async-start(bf16[128,8,1536]{2,1,0:T(8,128)(2,1)} %bitcast.10), calls=%async_computation.1 | async-start | bytes 6291456 | tf_op jit(solution)/shard_map/all_to_all | solution.py:307
  99.1 0.7 copy-start.4

commit v6 on v5

--- a/solution.py
+++ b/solution.py
@@ -121,11 +121,10 @@
     high = jnp.dot(high, spread, preferred_element_type=F32)
     low = jnp.dot(low, spread, preferred_element_type=F32)
     sub = iota((tok, cols), 1) & 7
-    for u in range(UNITS + 1):
+    for u in range(UNITS):
+        keep = (sub >= CAPE) & (rank == sub + (2 * u - CAPE))
         if u == 0:
-            keep = rank == sub
-        else:
-            keep = (sub >= CAPE) & (rank == sub + (2 * (u - 1) - CAPE))
+            keep = keep | (rank == sub)
         out_ref[2 * u * tok : (2 * u + 1) * tok, :] = jnp.where(keep, high, 0.0).astype(BF)
         out_ref[(2 * u + 1) * tok : (2 * u + 2) * tok, :] = jnp.where(keep, low, 0.0).astype(BF)
 
@@ -134,7 +133,7 @@
     tok = tokens.shape[0]
     return pl.pallas_call(
         gates_kernel,
-        out_shape=jax.ShapeDtypeStruct((2 * (UNITS + 1) * tok, EXPERTS * 8), BF),
+        out_shape=jax.ShapeDtypeStruct((2 * UNITS * tok, EXPERTS * 8), BF),
         in_specs=[VM, VM, VM],
         out_specs=VM,
         compiler_params=pltpu.CompilerParams(vmem_limit_bytes=16 << 20),
@@ -263,21 +262,33 @@
     )(x, w_in, w_out)
 
 
-def combine_kernel(gate_hbm, got_ref, out_ref, sum_ref, gate_ref, sem):
+def combine_kernel(gate_hbm, got_ref, out_ref, gate_ref, sem):
     tok = out_ref.shape[0]
     unit = got_ref.shape[2] // UNITS
-    load = pltpu.make_async_copy(gate_hbm, gate_ref, sem)
-    load.start()
-    sums = got_ref[:, :32, :].astype(F32) + got_ref[:, 32:, :].astype(F32)
-    sum_ref[...] = sums.astype(BF).reshape(sum_ref.shape)
-    load.wait()
-    main = gate_ref[0 : 2 * tok, :]
+    loads = []
+    for i, part in enumerate((slice(0, 2 * tok), slice(2 * tok, gate_ref.shape[0]))):
+        load = pltpu.make_async_copy(gate_hbm.at[part], gate_ref.at[part], sem.at[i])
+        load.start()
+        loads.append(load)
+    sums = []
+    for u in range(UNITS):
+        own = slice(u * unit, (u + 1) * unit)
+        added = got_ref[:, :32, own].astype(F32) + got_ref[:, 32:, own].astype(F32)
+        sums.append(added.astype(BF).reshape(-1, unit))
+    loads[0].wait()
+    both = gate_ref[0 : 2 * tok, :]
+    is_main = (iota(both.shape, 1) & 7) < CAPE
+    main = jnp.where(is_main, both, jnp.zeros_like(both))
+    tail = jnp.where(is_main, jnp.zeros_like(both), both)
     total = jnp.zeros((2 * tok, unit), F32)
     for u in range(UNITS):
-        tail = gate_ref[2 * tok * (u + 1) : 2 * tok * (u + 2), :]
+        if u == 1:
+            loads[1].wait()
+        if u > 0:
+            tail = gate_ref[2 * tok * u : 2 * tok * (u + 1), :]
         both = jnp.dot(
             jnp.concatenate([main, tail], axis=0),
-            sum_ref[:, u * unit : (u + 1) * unit],
+            sums[u],
             preferred_element_type=F32,
         )
         out_ref[:, u * unit : (u + 1) * unit] = (both[:tok] + both[tok : 2 * tok]).astype(BF)
@@ -286,16 +297,15 @@
 
 
 def combine(gate, got, tok, width):
-    rows, packed = got.shape
+    packed = got.shape[1]
     return pl.pallas_call(
         combine_kernel,
         out_shape=jax.ShapeDtypeStruct((tok, width), BF),
         in_specs=[pl.BlockSpec(memory_space=pltpu.HBM), VM],
         out_specs=VM,
         scratch_shapes=[
-            pltpu.VMEM((rows // 2, packed), BF),
             pltpu.VMEM(gate.shape, BF),
-            pltpu.SemaphoreType.DMA,
+            pltpu.SemaphoreType.DMA((2,)),
         ],
         compiler_params=pltpu.CompilerParams(vmem_limit_bytes=12 << 20),
         cost_estimate=pl.CostEstimate(flops=10**9, bytes_accessed=4 * 10**6, transcendentals=0),

time: 141 us -> 141 us (level)
  no operation moved by 1% of the time
where the time goes in v6:
time: 141 us
  waiting for transfers between devices  79.1 us (56%)
  Pallas kernels  31.2 us (22%)
  starting transfers between devices  22.6 us (16%)
  local copies, waits for them, and re-layouts  6.88 us (5%)
    all_to_all x3, waiting for transfers between devices, swap(): return lax.all_to_all(x, SWAP, split_axis=0, concat_axis=0, tiled=True)  79.1 us
    all_to_all x3, starting transfers between devices, swap(): return lax.all_to_all(x, SWAP, split_axis=0, concat_axis=0, tiled=True)  22.6 us
    pallas_call x1, Pallas kernels, experts(): pl.pallas_call(experts_kernel, grid=(rows // step,), out_shape=jax.ShapeD...  15.6 us
    pallas_call x1, Pallas kernels, pages_in(): pl.pallas_call(pages_in_kernel, out_shape=jax.ShapeDtypeStruct((pages, wi...  8.55 us
    unnamed x18, local copies, waits for them, and re-layouts  6.88 us
    pallas_call x1, Pallas kernels, dispatch(): pl.pallas_call(dispatch_kernel, out_shape=jax.ShapeDtypeStruct((16, 2, 32...  3.14 us
  transfers between devices with their start and end apart: 3, of which 3 were waited for; matrix products, arithmetic and copies ran while one was open for 0% of the time, Pallas kernels for 19%

profile of v6, /device:TPU:0, one launch (start us, length us, event | category | flops | bytes accessed | tf_op | source)
XLA Modules:
  0.0 140.8 jit_solution(17080035530834239740)
XLA Ops:
  0.6 3.1 %dispatch.1 = bf16[16,2,32,1536]{3,2,1,0:T(8,128)(2,1)} custom-call(s32[6,32]{1,0:T(8,128)} %bitcast.13, bf16[32,2048]{1,0:T(8,128)(2,1)} %tok_hbm.1), custom_call_target="tpu_custom_call" | custom-call | flops 100000000 | bytes 4000000 | tf_op jit(solution)/shard_map/dispatch/pallas_call | solution.py:79
  3.8 0.0 copy-start.8
  3.8 11.2 %all-to-all-start = ((bf16[128,8,1536]{2,1,0:T(8,128)(2,1)}), bf16[128,8,1536]{2,1,0:T(8,128)(2,1)S(1)}, u32[]{:S(2)}, u32[]{:S(2)}) async-start(bf16[128,8,1536]{2,1,0:T(8,128)(2,1)} %bitcast.17), calls=%async_computation | async-start | bytes 6291456 | tf_op jit(solution)/shard_map/all_to_all | solution.py:317
  14.9 0.0 copy-done.8
  15.0 0.0 copy-start.7
  15.0 1.3 copy-done.7
  16.3 1.4 %pages_out.1 = bf16[128,2,4736]{2,1,0:T(2,128)(2,1)S(1)} custom-call(s32[1,72]{1,0:T(1,128)S(1)} %bitcast.16, bf16[72,9216]{1,0:T(8,128)(2,1)S(1)} %copy-done.7), custom_call_target="tpu_custom_call" | custom-call | flops 2000000000 | bytes 4000000 | tf_op jit(solution)/shard_map/pages_out/pallas_call | solution.py:166
  17.7 0.0 copy-start.1
  17.7 1.4 %copy-done.1 = bf16[128,2,4736]{2,1,0:T(2,128)(2,1)} copy-done((bf16[128,2,4736]{2,1,0:T(2,128)(2,1)}, bf16[128,2,4736]{2,1,0:T(2,128)(2,1)S(1)}, u32[]{:S(2)}) %copy-start.1) | copy-done | bytes 2424856
  19.2 35.9 %all-to-all-done = bf16[128,8,1536]{2,1,0:T(8,128)(2,1)S(1)} async-done(((bf16[128,8,1536]{2,1,0:T(8,128)(2,1)}), bf16[128,8,1536]{2,1,0:T(8,128)(2,1)S(1)}, u32[]{:S(2)}, u32[]{:S(2)}) %all-to-all-start) | async-done | bytes 3145760 | tf_op jit(solution)/shard_map/all_to_all | solution.py:317
  55.1 5.8 %all-to-all-start.2 = ((bf16[128,2,4736]{2,1,0:T(2,128)(2,1)}), bf16[128,2,4736]{2,1,0:T(2,128)(2,1)}, u32[]{:S(2)}, u32[]{:S(2)}) async-start(bf16[128,2,4736]{2,1,0:T(2,128)(2,1)} %copy-done.1), calls=%async_computation.2 | async-start | bytes 4849664 | tf_op jit(solution)/shard_map/all_to_all | solution.py:317
  60.9 0.0 copy-start.6
  60.9 1.8 %copy-done.6 = bf16[1,704,2048]{2,1,0:T(8,128)(2,1)S(1)} copy-done((bf16[1,704,2048]{2,1,0:T(8,128)(2,1)S(1)}, bf16[1,704,2048]{2,1,0:T(8,128)(2,1)}, u32[]{:S(2)}) %copy-start.6) | copy-done | bytes 2883608
  62.8 15.6 %experts.1 = bf16[1024,1536]{1,0:T(8,128)(2,1)S(1)} custom-call(bf16[1024,1536]{1,0:T(8,128)(2,1)S(1)} %bitcast.9, bf16[2048,1408]{1,0:T(8,128)(2,1)} %bitcast.18, bf16[704,2048]{1,0:T(8,128)(2,1)S(1)} %bitcast.15), custom_call_target="tpu_custom_call" | custom-call | flops 10000000000 | bytes 15000000 | tf_op jit(solution)/shard_map/experts/pallas_call | solution.py:247
  78.3 0.0 copy-start
  78.4 1.6 %copy-done = bf16[1024,1536]{1,0:T(8,128)(2,1)} copy-done((bf16[1024,1536]{1,0:T(8,128)(2,1)}, bf16[1024,1536]{1,0:T(8,128)(2,1)S(1)}, u32[]{:S(2)}) %copy-start) | copy-done | bytes 3145752
  80.0 13.0 %all-to-all-done.2.got_ref = bf16[128,2,4736]{2,1,0:T(2,128)(2,1)} async-done(((bf16[128,2,4736]{2,1,0:T(2,128)(2,1)}), bf16[128,2,4736]{2,1,0:T(2,128)(2,1)}, u32[]{:S(2)}, u32[]{:S(2)}) %all-to-all-start.2) | async-done | bytes 2424864 | tf_op jit(solution)/shard_map/all_to_all | solution.py:317
  93.0 0.0 copy-start.2
  93.0 0.0 copy-start.3
  93.0 0.0 copy-start.5
  93.0 5.6 %all-to-all-start.1 = ((bf16[128,8,1536]{2,1,0:T(8,128)(2,1)}), bf16[128,8,1536]{2,1,0:T(8,128)(2,1)S(1)}, u32[]{:S(2)}, u32[]{:S(2)}) async-start(bf16[128,8,1536]{2,1,0:T(8,128)(2,1)} %bitcast.10), calls=%async_computation.1 | async-start | bytes 6291456 | tf_op jit(solution)/shard_map/all_to_all | solution.py:317
  98.6 0.0 copy-done.2
  98.6 0.0 copy-done.3
  98.6 0.0 copy-done.5
  98.6 0.5 gates.1.gate_hbm
  99.1 0.0 copy-start.4
  99.1 0.7 copy-done.4
  99.8 8.6 %pages_in.1 = bf16[72,9216]{1,0:T(8,128)(2,1)} custom-call(bf16[128,2,4736]{2,1,0:T(2,128)(2,1)} %all-to-all-done.2.got_ref), custom_call_target="tpu_custom_call" | custom-call | flops 2000000000 | bytes 4000000 | tf_op jit(solution)/shard_map/pages_in/pallas_call | solution.py:191
  108.4 30.2 %all-to-all-done.1 = bf16[128,8,1536]{2,1,0:T(8,128)(2,1)S(1)} async-done(((bf16[128,8,1536]{2,1,0:T(8,128)(2,1)}), bf16[128,8,1536]{2,1,0:T(8,128)(2,1)S(1)}, u32[]{:S(2)}, u32[]{:S(2)}) %all-to-all-start.1) | async-done | bytes 3145760 | tf_op jit(solution)/shard_map/all_to_all | solution.py:317
  138.6 2.1 %combine.1 = bf16[32,2048]{1,0:T(8,128)(2,1)} custom-call(bf16[192,512]{1,0:T(8,128)(2,1)} %copy-done.4, bf16[16,64,1536]{2,1,0:T(8,128)(2,1)S(1)} %bitcast.11), custom_call_target="tpu_custom_call" | custom-call | flops 1000000000 | bytes 4000000 | tf_op jit(solution)/shard_map/combine/pallas_call | solution.py:301
Async XLA Ops:
  3.8 11.2 %copy-start.8 = (s32[72]{0:T(128)S(1)}, s32[72]{0:T(128)}, u32[]{:S(2)}) copy-start(s32[72]{0:T(128)} %param.13) | copy-start | bytes 868
  3.8 51.3 %all-to-all-start = ((bf16[128,8,1536]{2,1,0:T(8,128)(2,1)}), bf16[128,8,1536]{2,1,0:T(8,128)(2,1)S(1)}, u32[]{:S(2)}, u32[]{:S(2)}) async-start(bf16[128,8,1536]{2,1,0:T(8,128)(2,1)} %bitcast.17), calls=%async_computation | async-start | bytes 6291456 | tf_op jit(solution)/shard_map/all_to_all | solution.py:317
  15.0 1.3 copy-start.7
  17.7 1.4 %copy-start.1 = (bf16[128,2,4736]{2,1,0:T(2,128)(2,1)}, bf16[128,2,4736]{2,1,0:T(2,128)(2,1)S(1)}, u32[]{:S(2)}) copy-start(bf16[128,2,4736]{2,1,0:T(2,128)(2,1)S(1)} %pages_out.1) | copy-start | bytes 7274500
  55.1 37.9 %all-to-all-start.2 = ((bf16[128,2,4736]{2,1,0:T(2,128)(2,1)}), bf16[128,2,4736]{2,1,0:T(2,128)(2,1)}, u32[]{:S(2)}, u32[]{:S(2)}) async-start(bf16[128,2,4736]{2,1,0:T(2,128)(2,1)} %copy-done.1), calls=%async_computation.2 | async-start | bytes 4849664 | tf_op jit(solution)/shard_map/all_to_all | solution.py:317
  60.9 1.8 %copy-start.6 = (bf16[1,704,2048]{2,1,0:T(8,128)(2,1)S(1)}, bf16[1,704,2048]{2,1,0:T(8,128)(2,1)}, u32[]{:S(2)}) copy-start(bf16[1,704,2048]{2,1,0:T(8,128)(2,1)} %param.11) | copy-start | bytes 8650756
  78.3 1.6 %copy-start = (bf16[1024,1536]{1,0:T(8,128)(2,1)}, bf16[1024,1536]{1,0:T(8,128)(2,1)S(1)}, u32[]{:S(2)}) copy-start(bf16[1024,1536]{1,0:T(8,128)(2,1)S(1)} %experts.1) | copy-start | bytes 9437188
  93.0 5.6 %copy-start.2 = (bf16[32,2048]{1,0:T(8,128)(2,1)S(1)}, bf16[32,2048]{1,0:T(8,128)(2,1)}, u32[]{:S(2)}) copy-start(bf16[32,2048]{1,0:T(8,128)(2,1)} %tok_hbm.1) | copy-start | bytes 393220
  93.0 5.6 %copy-start.3 = (bf16[2048,64]{0,1:T(8,128)(2,1)S(1)}, bf16[2048,64]{0,1:T(8,128)(2,1)}, u32[]{:S(2)}) copy-start(bf16[2048,64]{0,1:T(8,128)(2,1)} %param.9) | copy-start | bytes 786436
  93.0 5.6 %copy-start.5 = (s32[32,6]{0,1:T(8,128)S(1)}, s32[32,6]{0,1:T(8,128)}, u32[]{:S(2)}) copy-start(s32[32,6]{0,1:T(8,128)} %param.8) | copy-start | bytes 2308
  93.0 45.6 %all-to-all-start.1 = ((bf16[128,8,1536]{2,1,0:T(8,128)(2,1)}), bf16[128,8,1536]{2,1,0:T(8,128)(2,1)S(1)}, u32[]{:S(2)}, u32[]{:S(2)}) async-start(bf16[128,8,1536]{2,1,0:T(8,128)(2,1)} %bitcast.10), calls=%async_computation.1 | async-start | bytes 6291456 | tf_op jit(solution)/shard_map/all_to_all | solution.py:317
  99.1 0.7 copy-start.4

commit v7 on v6

--- a/solution.py
+++ b/solution.py
@@ -273,8 +273,7 @@
     sums = []
     for u in range(UNITS):
         own = slice(u * unit, (u + 1) * unit)
-        added = got_ref[:, :32, own].astype(F32) + got_ref[:, 32:, own].astype(F32)
-        sums.append(added.astype(BF).reshape(-1, unit))
+        sums.append((got_ref[:, :32, own] + got_ref[:, 32:, own]).reshape(-1, unit))
     loads[0].wait()
     both = gate_ref[0 : 2 * tok, :]
     is_main = (iota(both.shape, 1) & 7) < CAPE

time: 141 us -> 141 us (level)
  no operation moved by 1% of the time
where the time goes in v7:
time: 141 us
  waiting for transfers between devices  79.1 us (56%)
  Pallas kernels  31.2 us (22%)
  starting transfers between devices  22.6 us (16%)
  local copies, waits for them, and re-layouts  6.88 us (5%)
    all_to_all x3, waiting for transfers between devices, swap(): return lax.all_to_all(x, SWAP, split_axis=0, concat_axis=0, tiled=True)  79.1 us
    all_to_all x3, starting transfers between devices, swap(): return lax.all_to_all(x, SWAP, split_axis=0, concat_axis=0, tiled=True)  22.6 us
    pallas_call x1, Pallas kernels, experts(): pl.pallas_call(experts_kernel, grid=(rows // step,), out_shape=jax.ShapeD...  15.6 us
    pallas_call x1, Pallas kernels, pages_in(): pl.pallas_call(pages_in_kernel, out_shape=jax.ShapeDtypeStruct((pages, wi...  8.55 us
    unnamed x18, local copies, waits for them, and re-layouts  6.88 us
    pallas_call x1, Pallas kernels, dispatch(): pl.pallas_call(dispatch_kernel, out_shape=jax.ShapeDtypeStruct((16, 2, 32...  3.14 us
  transfers between devices with their start and end apart: 3, of which 3 were waited for; matrix products, arithmetic and copies ran while one was open for 0% of the time, Pallas kernels for 19%

profile of v7, /device:TPU:0, one launch (start us, length us, event | category | flops | bytes accessed | tf_op | source)
XLA Modules:
  0.0 140.8 jit_solution(16208504893771016963)
XLA Ops:
  0.6 3.1 %dispatch.1 = bf16[16,2,32,1536]{3,2,1,0:T(8,128)(2,1)} custom-call(s32[6,32]{1,0:T(8,128)} %bitcast.13, bf16[32,2048]{1,0:T(8,128)(2,1)} %tok_hbm.1), custom_call_target="tpu_custom_call" | custom-call | flops 100000000 | bytes 4000000 | tf_op jit(solution)/shard_map/dispatch/pallas_call | solution.py:79
  3.8 0.0 copy-start.8
  3.8 11.2 %all-to-all-start = ((bf16[128,8,1536]{2,1,0:T(8,128)(2,1)}), bf16[128,8,1536]{2,1,0:T(8,128)(2,1)S(1)}, u32[]{:S(2)}, u32[]{:S(2)}) async-start(bf16[128,8,1536]{2,1,0:T(8,128)(2,1)} %bitcast.17), calls=%async_computation | async-start | bytes 6291456 | tf_op jit(solution)/shard_map/all_to_all | solution.py:316
  14.9 0.0 copy-done.8
  15.0 0.0 copy-start.7
  15.0 1.3 copy-done.7
  16.3 1.4 %pages_out.1 = bf16[128,2,4736]{2,1,0:T(2,128)(2,1)S(1)} custom-call(s32[1,72]{1,0:T(1,128)S(1)} %bitcast.16, bf16[72,9216]{1,0:T(8,128)(2,1)S(1)} %copy-done.7), custom_call_target="tpu_custom_call" | custom-call | flops 2000000000 | bytes 4000000 | tf_op jit(solution)/shard_map/pages_out/pallas_call | solution.py:166
  17.7 0.0 copy-start.1
  17.7 1.4 %copy-done.1 = bf16[128,2,4736]{2,1,0:T(2,128)(2,1)} copy-done((bf16[128,2,4736]{2,1,0:T(2,128)(2,1)}, bf16[128,2,4736]{2,1,0:T(2,128)(2,1)S(1)}, u32[]{:S(2)}) %copy-start.1) | copy-done | bytes 2424856
  19.2 35.9 %all-to-all-done = bf16[128,8,1536]{2,1,0:T(8,128)(2,1)S(1)} async-done(((bf16[128,8,1536]{2,1,0:T(8,128)(2,1)}), bf16[128,8,1536]{2,1,0:T(8,128)(2,1)S(1)}, u32[]{:S(2)}, u32[]{:S(2)}) %all-to-all-start) | async-done | bytes 3145760 | tf_op jit(solution)/shard_map/all_to_all | solution.py:316
  55.1 5.8 %all-to-all-start.2 = ((bf16[128,2,4736]{2,1,0:T(2,128)(2,1)}), bf16[128,2,4736]{2,1,0:T(2,128)(2,1)}, u32[]{:S(2)}, u32[]{:S(2)}) async-start(bf16[128,2,4736]{2,1,0:T(2,128)(2,1)} %copy-done.1), calls=%async_computation.2 | async-start | bytes 4849664 | tf_op jit(solution)/shard_map/all_to_all | solution.py:316
  60.9 0.0 copy-start.6
  60.9 1.8 %copy-done.6 = bf16[1,704,2048]{2,1,0:T(8,128)(2,1)S(1)} copy-done((bf16[1,704,2048]{2,1,0:T(8,128)(2,1)S(1)}, bf16[1,704,2048]{2,1,0:T(8,128)(2,1)}, u32[]{:S(2)}) %copy-start.6) | copy-done | bytes 2883608
  62.8 15.6 %experts.1 = bf16[1024,1536]{1,0:T(8,128)(2,1)S(1)} custom-call(bf16[1024,1536]{1,0:T(8,128)(2,1)S(1)} %bitcast.9, bf16[2048,1408]{1,0:T(8,128)(2,1)} %bitcast.18, bf16[704,2048]{1,0:T(8,128)(2,1)S(1)} %bitcast.15), custom_call_target="tpu_custom_call" | custom-call | flops 10000000000 | bytes 15000000 | tf_op jit(solution)/shard_map/experts/pallas_call | solution.py:247
  78.3 0.0 copy-start
  78.4 1.6 %copy-done = bf16[1024,1536]{1,0:T(8,128)(2,1)} copy-done((bf16[1024,1536]{1,0:T(8,128)(2,1)}, bf16[1024,1536]{1,0:T(8,128)(2,1)S(1)}, u32[]{:S(2)}) %copy-start) | copy-done | bytes 3145752
  80.0 13.0 %all-to-all-done.2.got_ref = bf16[128,2,4736]{2,1,0:T(2,128)(2,1)} async-done(((bf16[128,2,4736]{2,1,0:T(2,128)(2,1)}), bf16[128,2,4736]{2,1,0:T(2,128)(2,1)}, u32[]{:S(2)}, u32[]{:S(2)}) %all-to-all-start.2) | async-done | bytes 2424864 | tf_op jit(solution)/shard_map/all_to_all | solution.py:316
  93.0 0.0 copy-start.2
  93.0 0.0 copy-start.3
  93.0 0.0 copy-start.5
  93.0 5.6 %all-to-all-start.1 = ((bf16[128,8,1536]{2,1,0:T(8,128)(2,1)}), bf16[128,8,1536]{2,1,0:T(8,128)(2,1)S(1)}, u32[]{:S(2)}, u32[]{:S(2)}) async-start(bf16[128,8,1536]{2,1,0:T(8,128)(2,1)} %bitcast.10), calls=%async_computation.1 | async-start | bytes 6291456 | tf_op jit(solution)/shard_map/all_to_all | solution.py:316
  98.6 0.0 copy-done.2
  98.6 0.0 copy-done.3
  98.6 0.0 copy-done.5
  98.6 0.5 gates.1.gate_hbm
  99.1 0.0 copy-start.4
  99.1 0.7 copy-done.4
  99.8 8.6 %pages_in.1 = bf16[72,9216]{1,0:T(8,128)(2,1)} custom-call(bf16[128,2,4736]{2,1,0:T(2,128)(2,1)} %all-to-all-done.2.got_ref), custom_call_target="tpu_custom_call" | custom-call | flops 2000000000 | bytes 4000000 | tf_op jit(solution)/shard_map/pages_in/pallas_call | solution.py:191
  108.4 30.2 %all-to-all-done.1 = bf16[128,8,1536]{2,1,0:T(8,128)(2,1)S(1)} async-done(((bf16[128,8,1536]{2,1,0:T(8,128)(2,1)}), bf16[128,8,1536]{2,1,0:T(8,128)(2,1)S(1)}, u32[]{:S(2)}, u32[]{:S(2)}) %all-to-all-start.1) | async-done | bytes 3145760 | tf_op jit(solution)/shard_map/all_to_all | solution.py:316
  138.6 2.0 %combine.1 = bf16[32,2048]{1,0:T(8,128)(2,1)} custom-call(bf16[192,512]{1,0:T(8,128)(2,1)} %copy-done.4, bf16[16,64,1536]{2,1,0:T(8,128)(2,1)S(1)} %bitcast.11), custom_call_target="tpu_custom_call" | custom-call | flops 1000000000 | bytes 4000000 | tf_op jit(solution)/shard_map/combine/pallas_call | solution.py:300
Async XLA Ops:
  3.8 11.2 %copy-start.8 = (s32[72]{0:T(128)S(1)}, s32[72]{0:T(128)}, u32[]{:S(2)}) copy-start(s32[72]{0:T(128)} %param.13) | copy-start | bytes 868
  3.8 51.3 %all-to-all-start = ((bf16[128,8,1536]{2,1,0:T(8,128)(2,1)}), bf16[128,8,1536]{2,1,0:T(8,128)(2,1)S(1)}, u32[]{:S(2)}, u32[]{:S(2)}) async-start(bf16[128,8,1536]{2,1,0:T(8,128)(2,1)} %bitcast.17), calls=%async_computation | async-start | bytes 6291456 | tf_op jit(solution)/shard_map/all_to_all | solution.py:316
  15.0 1.3 copy-start.7
  17.7 1.4 %copy-start.1 = (bf16[128,2,4736]{2,1,0:T(2,128)(2,1)}, bf16[128,2,4736]{2,1,0:T(2,128)(2,1)S(1)}, u32[]{:S(2)}) copy-start(bf16[128,2,4736]{2,1,0:T(2,128)(2,1)S(1)} %pages_out.1) | copy-start | bytes 7274500
  55.1 37.9 %all-to-all-start.2 = ((bf16[128,2,4736]{2,1,0:T(2,128)(2,1)}), bf16[128,2,4736]{2,1,0:T(2,128)(2,1)}, u32[]{:S(2)}, u32[]{:S(2)}) async-start(bf16[128,2,4736]{2,1,0:T(2,128)(2,1)} %copy-done.1), calls=%async_computation.2 | async-start | bytes 4849664 | tf_op jit(solution)/shard_map/all_to_all | solution.py:316
  60.9 1.8 %copy-start.6 = (bf16[1,704,2048]{2,1,0:T(8,128)(2,1)S(1)}, bf16[1,704,2048]{2,1,0:T(8,128)(2,1)}, u32[]{:S(2)}) copy-start(bf16[1,704,2048]{2,1,0:T(8,128)(2,1)} %param.11) | copy-start | bytes 8650756
  78.3 1.6 %copy-start = (bf16[1024,1536]{1,0:T(8,128)(2,1)}, bf16[1024,1536]{1,0:T(8,128)(2,1)S(1)}, u32[]{:S(2)}) copy-start(bf16[1024,1536]{1,0:T(8,128)(2,1)S(1)} %experts.1) | copy-start | bytes 9437188
  93.0 5.6 %copy-start.2 = (bf16[32,2048]{1,0:T(8,128)(2,1)S(1)}, bf16[32,2048]{1,0:T(8,128)(2,1)}, u32[]{:S(2)}) copy-start(bf16[32,2048]{1,0:T(8,128)(2,1)} %tok_hbm.1) | copy-start | bytes 393220
  93.0 5.6 %copy-start.3 = (bf16[2048,64]{0,1:T(8,128)(2,1)S(1)}, bf16[2048,64]{0,1:T(8,128)(2,1)}, u32[]{:S(2)}) copy-start(bf16[2048,64]{0,1:T(8,128)(2,1)} %param.9) | copy-start | bytes 786436
  93.0 5.6 %copy-start.5 = (s32[32,6]{0,1:T(8,128)S(1)}, s32[32,6]{0,1:T(8,128)}, u32[]{:S(2)}) copy-start(s32[32,6]{0,1:T(8,128)} %param.8) | copy-start | bytes 2308
  93.0 45.6 %all-to-all-start.1 = ((bf16[128,8,1536]{2,1,0:T(8,128)(2,1)}), bf16[128,8,1536]{2,1,0:T(8,128)(2,1)S(1)}, u32[]{:S(2)}, u32[]{:S(2)}) async-start(bf16[128,8,1536]{2,1,0:T(8,128)(2,1)} %bitcast.10), calls=%async_computation.1 | async-start | bytes 6291456 | tf_op jit(solution)/shard_map/all_to_all | solution.py:316
  99.1 0.7 copy-start.4
